TPU v7x, 32 devices: a whole 2x2x4 slice. The times are simulated.
32 devices in a mesh: fsdp: 4 (over y, x), ctx: 2 (over core), tp: 4 (over z).
Axes of the slice: x: 2, y: 2, z: 4, core: 2. Of those that a mesh axis runs over, the one named last changes fastest.
Arguments:
- tokens: bfloat16 [4, 2048, 1536], P('fsdp', 'ctx'), may hold values from -6 to 6
- segments: int32 [4, 2048], P('fsdp'), may hold values from 0 to 3, never falling along the last dimension, each value on 1 to 1024 neighbouring positions
- norm_gain: float32 [1536], replicated, may hold values from 0.5 to 1.5
- proj_main: bfloat16 [2, 1536, 3072], P(None, 'fsdp', 'tp'), may hold values from -0.15625 to 0.15625
- proj_shared: bfloat16 [1536, 256], P('fsdp'), may hold values from -0.15625 to 0.15625
- proj_step: bfloat16 [1536, 48], P('fsdp', 'tp'), may hold values from -0.15625 to 0.15625
- conv_main: float32 [5, 3072], P(None, 'tp'), may hold values from -0.5 to 0.5
- conv_shared: float32 [5, 256], replicated, may hold values from -0.5 to 0.5
- head_params: float32 [3, 48], P(None, 'tp'), may hold values from -7 to 2.1
- gate_gain: float32 [3072], P('tp'), may hold values from 0.5 to 1.5
- output_projection: bfloat16 [3072, 1536], P('tp', 'fsdp'), may hold values from -0.15625 to 0.15625
- cotangent: bfloat16 [4, 2048, 1536], P('fsdp', 'ctx'), may hold values from -6 to 6
Outputs:
- output: bfloat16 [4, 2048, 1536], P('fsdp', 'ctx', 'tp')
- grad_tokens: float32 [4, 2048, 1536], P('fsdp', 'ctx', 'tp')
- grad_norm_gain: float32 [1536], P('tp')
- grad_proj_main: float32 [2, 1536, 3072], P(None, ('fsdp', 'ctx'), 'tp')
- grad_proj_shared: float32 [1536, 256], P(('fsdp', 'ctx'))
- grad_proj_step: float32 [1536, 48], P(('fsdp', 'ctx'), 'tp')
- grad_conv_main: float32 [5, 3072], P(None, 'tp')
- grad_conv_shared: float32 [5, 256], replicated
- grad_head_params: float32 [3, 48], P(None, 'tp')
- grad_gate_gain: float32 [3072], P('tp')
- grad_proj_out: float32 [3072, 1536], P('tp', ('fsdp', 'ctx'))
Inputs may be any that keep to these rules, and one draw needn't show every extreme that they name: `segments`: never falling along a sequence; every sequence holds documents 0 to 3, each of 1 to 1024 positions, one of exactly 1024.
All inputs are finite; a program needn't handle non-finite values.
Results may differ from a plain program's by a relative error of at most 0.02.
Values may be sent and summed in bfloat16 or wider, within the bound.
No kernel may reach another device: no remote copies, remote signals or barrier semaphores. Data moves between devices by JAX's collectives and lax.ppermute only.
A program may use at most 192 MiB of HBM per device.

v0:
```python
import functools

import jax
import jax.numpy as jnp
from jax import lax
from jax.experimental import pallas as pl
from jax.experimental.pallas import tpu as pltpu
from jax.sharding import PartitionSpec as P


HEADDIM = 64
STATE = 128
STRETCH = 256
HALF = STRETCH // 2
INNER = 3072
EPSILON = 1e-05
HALO = 16
LANES = 128
SHARED = 2 * STATE
LEAD = SHARED + LANES
BF = jnp.bfloat16
F32 = jnp.float32
VMEM_LIMIT = 60 * 2**20


def dot_nn(a, b):
    return lax.dot_general(a, b, (((1,), (0,)), ((), ())), preferred_element_type=F32)


def dot_nt(a, b):
    return lax.dot_general(a, b, (((1,), (1,)), ((), ())), preferred_element_type=F32)


def dot_tn(a, b):
    return lax.dot_general(a, b, (((0,), (0,)), ((), ())), preferred_element_type=F32)


def split(v, n):
    terms = []
    for _ in range(n):
        high = v.astype(BF)
        terms.append(high)
        v = v - high.astype(F32)
    return terms


def exact(dot, a, b, n, left):
    total = None
    for term in split(a if left else b, n):
        part = dot(term, b) if left else dot(a, term)
        total = part if total is None else total + part
    return total


def iota(shape, axis):
    return lax.broadcasted_iota(jnp.int32, shape, axis)


def pair_widths(channels):
    return [(at, min(LANES, channels - at)) for at in range(0, channels, LANES)]


def spread(v, pair, width):
    first = v[:, 2 * pair : 2 * pair + 1]
    if width == HEADDIM:
        return jnp.broadcast_to(first, (v.shape[0], HEADDIM))
    second = v[:, 2 * pair + 1 : 2 * pair + 2]
    lane = iota((v.shape[0], LANES), 1)
    return jnp.where(lane < HEADDIM, first, second)


def head_masks(width):
    if width == HEADDIM:
        return [None]
    lane = iota((1, LANES), 1)
    return [(lane < HEADDIM).astype(F32).astype(BF), (lane >= HEADDIM).astype(F32).astype(BF)]


def masked(v, mask):
    return v if mask is None else v * mask


def sigmoid(v):
    return 1.0 / (1.0 + jnp.exp(-v))


def pack_in_kernel(shared_ref, step_ref, main_ref, out_ref):
    out_ref[:, 0:SHARED] = shared_ref[...]
    out_ref[:, SHARED:LEAD] = jnp.zeros((out_ref.shape[0], LANES), BF)
    out_ref[:, SHARED : SHARED + step_ref.shape[1]] = step_ref[...]
    out_ref[:, LEAD:] = main_ref[0]


def pack_go_kernel(main_ref, out_proj_ref, out_ref):
    channels = main_ref.shape[2]
    wide = out_ref.shape[1] // 2
    if wide != channels:
        out_ref[...] = jnp.zeros_like(out_ref)
    out_ref[:, 0:channels] = main_ref[0]
    out_ref[:, wide : wide + channels] = jnp.transpose(out_proj_ref[...].astype(F32)).astype(BF)


def fetches(idx_ref, pieces, held, sems, columns=None):
    own, near, near_other, far, far_other = pieces
    half = held.shape[1] // 2
    c = idx_ref[4]
    top, bottom = (pl.ds(pl.multiple_of(h * half, HALO), half) for h in (c, 1 - c))
    targets = (
        (own, held.at[idx_ref[0]]),
        (near, held.at[idx_ref[1]]),
        (near_other, held.at[idx_ref[2]]),
        (far, held.at[idx_ref[3], top]),
        (far_other, held.at[idx_ref[3], bottom]),
    )
    return [
        pltpu.make_async_copy(
            source if columns is None else source.at[:, columns], target, sems.at[i]
        )
        for i, (source, target) in enumerate(targets)
    ]


def fetch_all(copies):
    for copy in copies:
        copy.start()
    for copy in copies:
        copy.wait()


def prep_kernel(
    chunk, idx_ref, tok_ref, halo_ref, cot_ref, gain_ref, seg_ref, normed_ref, nhalo_ref, own_ref, owncot_ref,
    inv_ref, tab_ref,
):
    k = pl.program_id(0)

    def scale_of(x):
        return lax.rsqrt(jnp.mean(x * x, axis=-1, keepdims=True) + EPSILON)

    x = tok_ref[...].astype(F32)
    inv = scale_of(x)
    inv_ref[...] = jnp.broadcast_to(inv, inv_ref.shape)
    normed_ref[...] = (x * inv * gain_ref[0:1, :]).astype(BF)
    mine = pl.ds(pl.multiple_of(idx_ref[5] * chunk, LANES), chunk)
    own_ref[...] = tok_ref[:, mine]
    owncot_ref[...] = cot_ref[:, mine]

    @pl.when(k == 0)
    def _():
        x = halo_ref[...].astype(F32)
        nhalo_ref[...] = (x * scale_of(x) * gain_ref[0:1, :]).astype(BF)

    start = (idx_ref[4] * pl.num_programs(0) + k) * STRETCH
    here = seg_ref[0:1, pl.ds(pl.multiple_of(start, LANES), STRETCH)].astype(F32)
    before = seg_ref[0:1, pl.ds(pl.multiple_of(jnp.maximum(start - LANES, 0), LANES), LANES)].astype(F32)
    before = jnp.where(start == 0, -1.0, before)
    both = jnp.broadcast_to(jnp.concatenate([before, here], axis=1), (8, LANES + STRETCH))
    row = iota((8, STRETCH), 0)
    tab = both[:, LANES:]
    for j in (1, 2, 3):
        tab = jnp.where(row == j, pltpu.roll(both, j, 1)[:, LANES:], tab)
    tab = jnp.where(row == 4, before[:, LANES - 1 :], tab)
    tab_ref[...] = jnp.where(row == 5, here[:, STRETCH - 1 :], tab)


def columns_of(tab_ref):
    tab = tab_ref[...]
    row = iota(tab.shape, 0)
    test = jnp.where(tab == tab[0:1], 1.0, 0.0)
    value = jnp.where(row == 0, tab, test).astype(BF)
    eye = (iota((8, LANES), 0) == iota((8, LANES), 1)).astype(F32).astype(BF)
    return dot_tn(value, eye)


def load_heads(hp_ref, wide_ref):
    wide_ref[...] = jnp.zeros_like(wide_ref)
    wide_ref[0:3, 0 : hp_ref.shape[1]] = hp_ref[...]


def expand_of(channels):
    head = jnp.right_shift(iota((channels, LANES), 0), 6)
    return (head == iota((channels, LANES), 1)).astype(F32).astype(BF)


def skip_of(wide_ref, expand):
    return exact(dot_nt, jnp.broadcast_to(wide_ref[2:3, :], (8, LANES)), expand, 3, True)


def conv_taps(u, taps, masks):
    total = taps[4:5] + taps[3:4] * u[HALO:]
    for j in (1, 2, 3):
        total = total + taps[3 - j : 4 - j] * (pltpu.roll(u, j, 0)[HALO:] * masks[j - 1])
    return total


def act_and_slope(v):
    sig = sigmoid(v)
    act = v * sig
    return act, sig + act * (1.0 - sig)


def first_kernel(
    idx_ref, own_ref, near_ref, nearx_ref, far_ref, farx_ref, normed_ref, nhalo_ref, km_ref, ks_ref, heads_ref, tab_ref,
    pre_ref, phalo_ref, x_ref, xs_ref, slope_ref, bc_ref, slopes_ref, step_ref, cum_ref, sgm_ref, state_ref, fac_ref,
    total_ref,
    held, sems, edge, carry, hp_ref, expand_ref,
):
    k = pl.program_id(0)
    channels = x_ref.shape[1]
    count, chunk = held.shape[0], held.shape[1]

    def project(rows):
        total = dot_nn(rows[:, :chunk], held[0])
        for a in range(1, count):
            total = total + dot_nn(rows[:, a * chunk : (a + 1) * chunk], held[a])
        return total.astype(BF)

    @pl.when(k == 0)
    def _():
        copies = fetches(idx_ref, (own_ref, near_ref, nearx_ref, far_ref, farx_ref), held, sems)
        for copy in copies:
            copy.start()
        carry[...] = jnp.zeros_like(carry)
        load_heads(heads_ref, hp_ref)
        expand_ref[...] = expand_of(channels)
        for copy in copies:
            copy.wait()
        before = project(nhalo_ref[...])
        phalo_ref[...] = before
        edge[...] = before

    pre_ref[...] = project(normed_ref[...])

    def ext(lanes):
        return jnp.concatenate([edge[:, lanes].astype(F32), pre_ref[:, lanes].astype(F32)], axis=0)

    col = columns_of(tab_ref)
    masks = [col[:, j : j + 1] for j in (1, 2, 3)]
    alive, ends = col[:, 4:5], col[:, 5:6]

    raw = pre_ref[:, SHARED:LEAD].astype(F32)
    pre = raw + hp_ref[1:2, :]
    soft = jnp.exp(-jnp.abs(pre))
    step = jnp.maximum(pre, 0.0) + jnp.log1p(soft)
    step_ref[...] = step
    sgm_ref[...] = sigmoid(pre)
    log_decay = step * -jnp.exp(hp_ref[0:1, :])
    tri = (iota((STRETCH, STRETCH), 0) >= iota((STRETCH, STRETCH), 1)).astype(F32).astype(BF)
    cum = exact(dot_nn, tri, log_decay, 3, False)
    cum_ref[...] = cum
    last = cum[STRETCH - 1 : STRETCH]
    ef = jnp.exp(last - cum) * ends
    factor = jnp.exp(last) * alive[STRETCH - 1 : STRETCH]
    fac_row = exact(dot_nt, jnp.broadcast_to(factor, (8, LANES)), expand_ref[...], 3, True)
    fac_ref[0] = fac_row

    acts, slopes = act_and_slope(
        conv_taps(ext(slice(0, SHARED)), ks_ref[...], masks)
    )
    bc_ref[...] = acts.astype(BF)
    slopes_ref[...] = slopes.astype(BF)
    keys_t = jnp.transpose(acts[:, 0:STATE]).astype(BF)
    for pair, (at, width) in enumerate(pair_widths(channels)):
        lanes = slice(at, at + width)
        u = ext(slice(LEAD + at, LEAD + at + width))
        act, slope = act_and_slope(conv_taps(u, km_ref[:, lanes], masks))
        low = act.astype(BF)
        x_ref[:, lanes] = low
        slope_ref[:, lanes] = slope.astype(BF)
        xs = (low.astype(F32) * spread(step, pair, width)).astype(BF)
        xs_ref[:, lanes] = xs
        xe = (xs.astype(F32) * spread(ef, pair, width)).astype(BF)
        state = dot_nn(keys_t, xe)
        state_ref[0, :, lanes] = state
        carry[:, lanes] = carry[:, lanes] * fac_row[0:1, lanes] + state

    edge[...] = pre_ref[STRETCH - HALO :, :]

    @pl.when(k == pl.num_programs(0) - 1)
    def _():
        total_ref[...] = carry[...].astype(BF)


def doc_mask(seg_col, seg_row, shape, transposed):
    down, across = iota(shape, 0), iota(shape, 1)
    order = (across >= down) if transposed else (down >= across)
    return (seg_col == seg_row) & order


def second_kernel(
    bc_ref, x_ref, xs_ref, cum_ref, state_ref, fac_ref, enter_ref, heads_ref, tab_ref,
    y_ref, hist_ref,
    hold, hp_ref, skip_ref,
):
    k = pl.program_id(0)
    channels = x_ref.shape[1]

    @pl.when(k == 0)
    def _():
        hold[...] = enter_ref[...].astype(F32)
        load_heads(heads_ref, hp_ref)
        skip_ref[...] = skip_of(hp_ref, expand_of(channels))

    hist_ref[pl.ds(k, 1)] = hold[...].astype(BF)[None]
    col = columns_of(tab_ref)
    alive = col[:, 4:5]
    keys, queries = bc_ref[:, 0:STATE], bc_ref[:, STATE:SHARED]
    gram = dot_nt(queries, keys)
    valid = doc_mask(col[:, 0:1], tab_ref[0:1, :], (STRETCH, STRETCH), False)
    gram = jnp.where(valid, gram, 0.0)
    cum = cum_ref[...]
    cum_t = jnp.transpose(cum)
    rise = jnp.exp(cum) * alive
    for pair, (at, width) in enumerate(pair_widths(channels)):
        lanes = slice(at, at + width)
        xs = xs_ref[:, lanes]
        top = bottom = 0.0
        for which, mask in enumerate(head_masks(width)):
            h = 2 * pair + which
            here = masked(xs, mask)
            down, across = cum[:, h : h + 1], cum_t[h : h + 1, :]
            decay = jnp.exp(jnp.minimum(down[:HALF] - across[:, :HALF], 0.0))
            top = top + dot_nn((decay * gram[:HALF, :HALF]).astype(BF), here[:HALF])
            decay = jnp.exp(jnp.minimum(down[HALF:] - across, 0.0))
            bottom = bottom + dot_nn((decay * gram[HALF:]).astype(BF), here)
        within = jnp.concatenate([top, bottom], axis=0)
        old = hold[:, lanes]
        carried = dot_nn(queries, old.astype(BF)) * spread(rise, pair, width)
        hold[:, lanes] = old * fac_ref[0, 0:1, lanes] + state_ref[0, :, lanes]
        y = within + carried + skip_ref[0:1, lanes] * x_ref[:, lanes].astype(F32)
        y_ref[:, lanes] = y

    @pl.when(k == pl.num_programs(0) - 1)
    def _():
        hist_ref[pl.ds(k + 1, 1)] = hold[...].astype(BF)[None]


def gate_kernel(
    idx_ref, own_ref, near_ref, nearx_ref, far_ref, farx_ref, normed_ref, y_ref, cot_ref, gain_ref,
    gate_ref, gg_ref, out0_ref, out1_ref, out2_ref, out3_ref, stat_ref,
    held, sems,
):
    k = pl.program_id(0)
    channels = y_ref.shape[1]
    count, chunk = held.shape[0], held.shape[1]
    at_out = held.shape[2] // 2

    @pl.when(k == 0)
    def _():
        fetch_all(fetches(idx_ref, (own_ref, near_ref, nearx_ref, far_ref, farx_ref), held, sems))

    gates = dot_nn(normed_ref[:, :chunk], held[0, :, 0:channels])
    for a in range(1, count):
        gates = gates + dot_nn(normed_ref[:, a * chunk : (a + 1) * chunk], held[a, :, 0:channels])
    gate_ref[...] = gates.astype(BF)
    square = jnp.zeros((STRETCH, LANES), F32)
    for at, width in pair_widths(channels):
        lanes = slice(at, at + width)
        gate = gate_ref[:, lanes].astype(F32)
        gated = y_ref[:, lanes] * (gate * sigmoid(gate))
        gg_ref[:, lanes] = (gated * gain_ref[0:1, lanes]).astype(BF)
        square = square + padded(gated * gated)
    cross = jnp.zeros((STRETCH, LANES), F32)
    for q, out_ref in enumerate((out0_ref, out1_ref, out2_ref, out3_ref)):
        a = lax.rem(idx_ref[6] + q, count)
        out = dot_nt(gg_ref[...], held[a, :, at_out : at_out + channels])
        out_ref[...] = out.astype(BF)
        inner = out * cot_ref[:, pl.ds(pl.multiple_of(a * chunk, LANES), chunk)].astype(F32)
        for part in range(0, chunk, LANES):
            cross = cross + inner[:, part : part + LANES]
    ones = jnp.ones((8, LANES), BF)
    square = exact(dot_nt, ones, square, 3, False)
    cross = exact(dot_nt, ones, cross, 3, False)
    stat_ref[...] = jnp.where(iota((8, STRETCH), 0) == 0, square, cross)


def padded(v):
    if v.shape[1] == LANES:
        return v
    return jnp.concatenate([v, jnp.zeros((v.shape[0], LANES - v.shape[1]), v.dtype)], axis=1)


def gng_kernel(idx_ref, own_ref, near_ref, nearx_ref, far_ref, farx_ref, cot_ref, gng_ref, held, sems):
    count, chunk = held.shape[0], held.shape[1]
    channels = gng_ref.shape[1]

    @pl.when(pl.program_id(0) == 0)
    def _():
        out = pl.ds(own_ref.shape[1] // 2, held.shape[2])
        fetch_all(fetches(idx_ref, (own_ref, near_ref, nearx_ref, far_ref, farx_ref), held, sems, out))

    total = dot_nn(cot_ref[:, :chunk], held[0, :, 0:channels])
    for a in range(1, count):
        total = total + dot_nn(cot_ref[:, a * chunk : (a + 1) * chunk], held[a, :, 0:channels])
    gng_ref[...] = total.astype(BF)


def third_kernel(
    stat_ref, y_ref, gate_ref, gng_ref, gain_ref, bc_ref, cum_ref, fac_ref, tab_ref,
    gy_ref, gi_ref, inv_ref, flow_ref, gaingrad_ref,
    hold,
):
    i = pl.program_id(0)
    channels = y_ref.shape[1]

    @pl.when(i == 0)
    def _():
        hold[...] = jnp.zeros_like(hold)
        gaingrad_ref[...] = jnp.zeros_like(gaingrad_ref)

    pick = iota((8, LANES), 0)
    stat = stat_ref[...]
    square = exact(dot_tn, stat, (pick == 0).astype(F32).astype(BF), 3, True)
    cross = exact(dot_tn, stat, (pick == 1).astype(F32).astype(BF), 3, True)
    inv = lax.rsqrt(square / INNER + EPSILON)
    inv_ref[...] = inv
    back = inv * inv * inv * (cross / INNER)
    rise = jnp.exp(cum_ref[...]) * columns_of(tab_ref)[:, 4:5]
    queries_t = jnp.transpose(bc_ref[:, STATE:SHARED].astype(F32)).astype(BF)
    for pair, (at, width) in enumerate(pair_widths(channels)):
        lanes = slice(at, at + width)
        gate = gate_ref[:, lanes].astype(F32)
        act, slope = act_and_slope(gate)
        y = y_ref[:, lanes]
        gated = y * act
        gng = gng_ref[:, lanes].astype(F32)
        along = inv[:, :width]
        grad = along * (gain_ref[0:1, lanes] * gng) - gated * back[:, :width]
        gaingrad_ref[0:1, lanes] += jnp.sum(gng * gated * along, axis=0, keepdims=True)
        gy = (grad * act).astype(BF)
        gy_ref[:, lanes] = gy
        gi_ref[:, lanes] = (grad * y * slope).astype(BF)
        gyr = (gy.astype(F32) * spread(rise, pair, width)).astype(BF)
        hold[:, lanes] = dot_nn(queries_t, gyr) + fac_ref[0, 0:1, lanes] * hold[:, lanes]

    @pl.when(i == pl.num_programs(0) - 1)
    def _():
        flow_ref[...] = hold[...].astype(BF)


def conv_back(post, u, taps, masks, kgrad_ref, lanes):
    full = post.shape[0] + HALO
    pad = jnp.zeros((HALO, post.shape[1]), F32)
    total = jnp.concatenate([pad, post * taps[3:4]], axis=0)
    kgrad_ref[4:5, lanes] += jnp.sum(post, axis=0, keepdims=True)
    kgrad_ref[3:4, lanes] += jnp.sum(post * u[HALO:], axis=0, keepdims=True)
    for j in (1, 2, 3):
        here = post * masks[j - 1]
        kgrad_ref[3 - j : 4 - j, lanes] += jnp.sum(
            here * pltpu.roll(u, j, 0)[HALO:], axis=0, keepdims=True
        )
        wide = jnp.concatenate([pad, here * taps[3 - j : 4 - j]], axis=0)
        total = total + pltpu.roll(wide, full - j, 0)
    return total


def fourth_kernel(
    idx_ref, own_ref, near_ref, nearx_ref, far_ref, farx_ref,
    gy_ref, x_ref, xs_ref, slope_ref, y_ref, bc_ref, slopes_ref, step_ref, cum_ref, sgm_ref, pre_ref, prev_ref,
    phalo_ref, ht_ref, hn_ref, fac_ref, enter_ref, km_ref, ks_ref, heads_ref, tab_ref, gategrad_ref,
    g_ref, ghalo_ref, small_ref, back_ref,
    held, sems, hold, edge, hp_ref, expand_ref, skip_ref, skipgrad_ref, kmgrad_ref, ksgrad_ref, head_ref,
):
    i = pl.program_id(0)
    k = pl.num_programs(0) - 1 - i
    channels = x_ref.shape[1]
    copies = fetches(idx_ref, (own_ref, near_ref, nearx_ref, far_ref, farx_ref), held, sems)

    @pl.when(i == 0)
    def _():
        for copy in copies:
            copy.start()
        hold[...] = enter_ref[...].astype(F32)
        edge[...] = jnp.zeros_like(edge)
        load_heads(heads_ref, hp_ref)
        expand_ref[...] = expand_of(channels)
        skip_ref[...] = skip_of(hp_ref, expand_ref[...])
        kmgrad_ref[...] = jnp.zeros_like(kmgrad_ref)
        ksgrad_ref[...] = jnp.zeros_like(ksgrad_ref)
        head_ref[...] = jnp.zeros_like(head_ref)
        skipgrad_ref[...] = jnp.zeros_like(skipgrad_ref)

    def ext(lanes):
        before = jnp.where(k == 0, phalo_ref[:, lanes].astype(F32), prev_ref[:, lanes].astype(F32))
        return jnp.concatenate([before, pre_ref[:, lanes].astype(F32)], axis=0)

    def put(lanes, total):
        g_ref[0 : STRETCH - HALO, lanes] = total[HALO:STRETCH].astype(BF)
        g_ref[STRETCH - HALO :, lanes] = (total[STRETCH:] + edge[:, lanes]).astype(BF)
        edge[:, lanes] = total[:HALO]

    col = columns_of(tab_ref)
    masks = [col[:, j : j + 1] for j in (1, 2, 3)]
    alive, ends = col[:, 4:5], col[:, 5:6]
    keys, queries = bc_ref[:, 0:STATE], bc_ref[:, STATE:SHARED]
    queries_t = jnp.transpose(queries.astype(F32)).astype(BF)
    valid = doc_mask(col[:, 0:1], tab_ref[0:1, :], (STRETCH, STRETCH), True)
    gram = jnp.where(valid, dot_nt(keys, queries), 0.0)
    step, cum = step_ref[...], cum_ref[...]
    cum_t = jnp.transpose(cum)
    rise = jnp.exp(cum) * alive
    ef = jnp.exp(cum[STRETCH - 1 : STRETCH] - cum) * ends
    gram_top = jnp.zeros((HALF, STRETCH), F32)
    gram_bottom = jnp.zeros((HALF, HALF), F32)
    grad_keys = jnp.zeros((STRETCH, STATE), F32)
    grad_queries = jnp.zeros((STRETCH, STATE), F32)
    rowterm = jnp.zeros((STRETCH, LANES), F32)
    colterm = jnp.zeros((STRETCH, LANES), F32)
    endterm = jnp.zeros((8, LANES), F32)
    for pair, (at, width) in enumerate(pair_widths(channels)):
        lanes = slice(at, at + width)
        expand = expand_ref[lanes, :]
        gy, xs = gy_ref[:, lanes], xs_ref[:, lanes]
        gyf, xf = gy.astype(F32), x_ref[:, lanes].astype(F32)
        skip = skip_ref[0:1, lanes]
        top = bottom = 0.0
        for which, mask in enumerate(head_masks(width)):
            h = 2 * pair + which
            here = masked(gy, mask)
            down, across = cum[:, h : h + 1], cum_t[h : h + 1, :]
            decay = jnp.exp(jnp.minimum(across - down[:HALF], 0.0))
            top = top + dot_nn((decay * gram[:HALF]).astype(BF), here)
            gram_top = gram_top + dot_nt(xs[:HALF], here) * decay
            decay = jnp.exp(jnp.minimum(across[:, HALF:] - down[HALF:], 0.0))
            bottom = bottom + dot_nn((decay * gram[HALF:, HALF:]).astype(BF), here[HALF:])
            gram_bottom = gram_bottom + dot_nt(xs[HALF:], here[HALF:]) * decay
        grad_xs = jnp.concatenate([top, bottom], axis=0)
        after = hold[:, lanes]
        low = after.astype(BF)
        efs = spread(ef, pair, width)
        grad_xs = grad_xs + dot_nn(keys, low) * efs
        gyr = (gyf * spread(rise, pair, width)).astype(BF)
        xe = (xs.astype(F32) * efs).astype(BF)
        grad_queries = grad_queries + dot_nt(gyr, ht_ref[0, :, lanes])
        grad_keys = grad_keys + dot_nt(xe, low)
        ended = jnp.sum(after * hn_ref[0, :, lanes].astype(F32), axis=0, keepdims=True)
        endterm = endterm + exact(dot_nn, jnp.broadcast_to(ended, (8, width)), expand, 3, True)
        hold[:, lanes] = dot_nn(queries_t, gyr) + fac_ref[0, 0:1, lanes] * after
        rowterm = rowterm + exact(dot_nn, gyf * (y_ref[:, lanes] - skip * xf), expand, 2, True)
        colterm = colterm + exact(dot_nn, xf * grad_xs, expand, 2, True)
        skipgrad_ref[0:1, lanes] += jnp.sum(gyf * xf, axis=0, keepdims=True)
        grad_x = grad_xs * spread(step, pair, width) + skip * gyf
        post = grad_x * slope_ref[:, lanes].astype(F32)
        at_g = slice(LEAD + at, LEAD + at + width)
        put(at_g, conv_back(post, ext(at_g), km_ref[:, lanes], masks, kmgrad_ref, lanes))

    gram_top = jnp.where(valid[:HALF], gram_top, 0.0).astype(BF)
    gram_bottom = jnp.where(valid[HALF:, HALF:], gram_bottom, 0.0).astype(BF)
    grad_keys = grad_keys + jnp.concatenate(
        [dot_nn(gram_top, queries), dot_nn(gram_bottom, queries[HALF:])], axis=0
    )
    lower = jnp.concatenate([jnp.zeros((HALF, HALF), BF), gram_bottom], axis=1)
    gram_all = jnp.concatenate([gram_top, lower], axis=0)
    grad_queries = grad_queries + dot_tn(gram_all, keys)
    post = jnp.concatenate([grad_keys, grad_queries], axis=1) * slopes_ref[...].astype(F32)
    shared = slice(0, SHARED)
    put(shared, conv_back(post, ext(shared), ks_ref[...], masks, ksgrad_ref, shared))

    rate = -jnp.exp(hp_ref[0:1, :])
    grad_cum = rowterm - step * colterm
    at_end = iota((STRETCH, LANES), 0) == STRETCH - 1
    grad_cum = grad_cum + jnp.where(at_end, endterm[0:1], 0.0)
    upper = (iota((STRETCH, STRETCH), 1) >= iota((STRETCH, STRETCH), 0)).astype(F32).astype(BF)
    grad_log = exact(dot_nn, upper, grad_cum, 3, False)
    grad_pre = (colterm + grad_log * rate) * sgm_ref[...]
    g_ref[:, SHARED:LEAD] = grad_pre.astype(BF)
    head_ref[0:1, :] += jnp.sum(grad_log * step, axis=0, keepdims=True) * rate
    head_ref[1:2, :] += jnp.sum(grad_pre, axis=0, keepdims=True)

    @pl.when(k == 0)
    def _():
        ghalo_ref[:, 0:SHARED] = edge[:, 0:SHARED].astype(BF)
        ghalo_ref[:, LEAD:] = edge[:, LEAD:].astype(BF)
        ghalo_ref[:, SHARED:LEAD] = jnp.zeros((HALO, LANES), BF)
        wide = jnp.broadcast_to(skipgrad_ref[0:1, :], (8, channels))
        small_ref[...] = jnp.zeros_like(small_ref)
        small_ref[1:6, 0:channels] = kmgrad_ref[0:5, :]
        small_ref[6:11, 0:SHARED] = ksgrad_ref[0:5, :]
        small_ref[11:12, 0:channels] = gategrad_ref[0:1, :]
        small_ref[12:14, 0:LANES] = head_ref[0:2, :]
        small_ref[14:15, 0:LANES] = exact(dot_nn, wide, expand_ref[...], 3, True)[0:1]
        for copy in copies:
            copy.wait()
        chunk = held.shape[1]
        for a in range(held.shape[0]):
            back_ref[:, a * chunk : (a + 1) * chunk] = dot_nt(ghalo_ref[...], held[a])


def normed_kernel(
    idx_ref, own0_ref, near0_ref, nearx0_ref, far0_ref, farx0_ref, own_ref, near_ref, nearx_ref, far_ref, farx_ref,
    gi_ref, g_ref, normed_ref, back_ref, small_ref,
    out0_ref, out1_ref, out2_ref, out3_ref, cross_ref, sums_ref,
    held0, held, sems0, sems, acc,
):
    i = pl.program_id(0)
    last = i == pl.num_programs(0) - 1
    rows = gi_ref.shape[0]
    count, chunk, channels = held0.shape

    @pl.when(i == 0)
    def _():
        pieces = (own0_ref, near0_ref, nearx0_ref, far0_ref, farx0_ref)
        columns = pl.ds(0, channels)
        copies = fetches(idx_ref, pieces, held0, sems0, columns)
        copies += fetches(idx_ref, (own_ref, near_ref, nearx_ref, far_ref, farx_ref), held, sems)
        fetch_all(copies)
        sums_ref[...] = small_ref[...]

    cross = jnp.zeros((rows, LANES), F32)
    for q, out_ref in enumerate((out0_ref, out1_ref, out2_ref, out3_ref)):
        a = lax.rem(idx_ref[6] + q, count)
        lanes = pl.ds(pl.multiple_of(a * chunk, LANES), chunk)
        width = gi_ref.shape[1]
        acc[...] = dot_nt(gi_ref[...], held0[a, :, 0:width]) + dot_nt(g_ref[...], held[a])

        @pl.when(last)
        def _():
            acc[rows - HALO :, :] += back_ref[:, lanes]

        total = acc[...]
        out_ref[...] = total.astype(BF)
        inner = total * normed_ref[:, lanes].astype(F32)
        sums_ref[0:1, lanes] += jnp.sum(inner, axis=0, keepdims=True)
        for part in range(0, chunk, LANES):
            cross = cross + inner[:, part : part + LANES]
    cross_ref[...] = exact(dot_nt, jnp.ones((8, LANES), BF), cross, 3, False)


def put_chunk(idx_ref, keep_ref, send_ref, lanes, value):
    j = pl.program_id(0)
    half = keep_ref.shape[1]
    top, bottom = value[:half].astype(BF), value[half:].astype(BF)

    @pl.when(j == idx_ref[1])
    def _():
        keep_ref[0, :, lanes] = top
        keep_ref[1, :, lanes] = bottom

    @pl.when(j == idx_ref[2])
    def _():
        send_ref[0, :, lanes] = top
        send_ref[1, :, lanes] = bottom

    for source, target in ((0, 3), (3, 2)):
        for c, (mine, other) in enumerate(((top, bottom), (bottom, top))):

            @pl.when((j == idx_ref[source]) & (idx_ref[4] == c))
            def _():
                keep_ref[target, :, lanes] = mine
                send_ref[target, :, lanes] = other


def weight_kernel(idx_ref, normed_ref, nhalo_ref, g_ref, ghalo_ref, keep_ref, send_ref):
    value = dot_tn(normed_ref[...], g_ref[...]) + dot_tn(nhalo_ref[...], ghalo_ref[...])
    put_chunk(idx_ref, keep_ref, send_ref, slice(None), value)


def gate_out_kernel(idx_ref, normed_ref, gi_ref, cot_ref, inv_ref, gg_ref, keep_ref, send_ref):
    channels = gi_ref.shape[1]
    wide = keep_ref.shape[2] // 2
    put_chunk(idx_ref, keep_ref, send_ref, slice(0, channels), dot_tn(normed_ref[...], gi_ref[...]))
    scaled = [
        (cot_ref[:, at : at + LANES].astype(F32) * inv_ref[...]).astype(BF)
        for at in range(0, cot_ref.shape[1], LANES)
    ]
    value = dot_tn(jnp.concatenate(scaled, axis=1), gg_ref[...])
    put_chunk(idx_ref, keep_ref, send_ref, slice(wide, wide + channels), value)


def output_kernel(own_ref, inv_ref, part_ref, right_ref, left_ref, out_ref):
    inv = inv_ref[...]
    for at in range(0, out_ref.shape[1], LANES):
        lanes = slice(at, at + LANES)
        total = part_ref[:, lanes].astype(F32) + right_ref[:, lanes].astype(F32)
        total = (total + left_ref[:, lanes].astype(F32)) * inv
        out_ref[:, lanes] = (own_ref[:, lanes].astype(F32) + total).astype(BF)


def tokens_kernel(
    width, own_ref, cot_ref, inv_ref, cross_ref, gain_ref, part_ref, right_ref, left_ref, out_ref
):
    inv = inv_ref[...]
    pick = (iota((8, LANES), 0) == 0).astype(F32).astype(BF)
    cross = exact(dot_tn, cross_ref[...], pick, 3, True)
    back = inv * inv * (cross / width)
    for at in range(0, out_ref.shape[1], LANES):
        lanes = slice(at, at + LANES)
        total = part_ref[:, lanes].astype(F32) + right_ref[:, lanes].astype(F32)
        total = total + left_ref[:, lanes].astype(F32)
        out_ref[:, lanes] = (
            inv * gain_ref[0:1, lanes] * total
            - own_ref[:, lanes].astype(F32) * back
            + cot_ref[:, lanes].astype(F32)
        )


def whole(array):
    rank = len(array.shape)
    return pl.BlockSpec(array.shape, lambda *_: (0,) * rank)


def call(kernel, grid, ins, in_specs, outs, out_specs, scratch=(), flops=0, prefetch=0):
    moved = sum(a.size * a.dtype.itemsize for a in (*ins, *outs))
    return pl.pallas_call(
        kernel,
        out_shape=outs,
        grid_spec=pltpu.PrefetchScalarGridSpec(
            num_scalar_prefetch=prefetch,
            grid=grid,
            in_specs=in_specs,
            out_specs=out_specs,
            scratch_shapes=list(scratch),
        ),
        compiler_params=pltpu.CompilerParams(
            dimension_semantics=("arbitrary",) * len(grid), vmem_limit_bytes=VMEM_LIMIT
        ),
        cost_estimate=pl.CostEstimate(
            flops=int(flops), bytes_accessed=int(moved), transcendentals=0
        ),
    )(*ins)


def shape(dims, kind):
    return jax.ShapeDtypeStruct(dims, kind)


def add(*terms):
    return sum(term.astype(F32) for term in terms).astype(BF)


def per_device(
    tokens, segments, norm_gain, proj_main, proj_shared, proj_step, conv_main, conv_shared,
    head_params, gate_gain, output_projection, cotangent,
):
    _, length, width = tokens.shape
    nf, nc, nt = lax.axis_size("fsdp"), lax.axis_size("ctx"), lax.axis_size("tp")
    assert nf == 4 and nc == 2
    f, c, t = lax.axis_index("fsdp"), lax.axis_index("ctx"), lax.axis_index("tp")
    heads = head_params.shape[1]
    channels = heads * HEADDIM
    lead = LEAD + channels
    wide = -(-channels // LANES) * LANES
    nb = length // STRETCH
    chunk = width // nf
    half = chunk // 2
    share = width // nt
    line = nt == nf
    rot = t if line else jnp.zeros_like(t)
    both = ("fsdp", "ctx")
    spots = [(i, j) for i in range(nf) for j in range(nc)]
    role = [(i * nc + j, (i ^ (1 + j)) * nc + j) for i, j in spots]
    turn = [(i * nc + j, (i ^ (2 - j)) * nc + j) for i, j in spots]
    across_chip = [(i * nc + j, (i ^ 3) * nc + j) for i, j in spots]
    swap = [(0, 1), (1, 0)]
    idx = jnp.stack([f, f ^ (1 + c), f ^ (2 - c), f ^ 3, c, rot, rot, rot]).astype(jnp.int32)

    def tp_sum(v):
        if not line:
            return lax.psum(v, "tp")
        first, second, third = (
            lax.ppermute(v, "tp", [(i, i ^ m) for i in range(nt)]) for m in (1, 2, 3)
        )
        return (v + first) + (second + third)

    def one(v, at):
        return lax.dynamic_slice_in_dim(v, at, 1, 0)

    def gather_rows(shard, direct):
        columns = shard.shape[1]
        pieces = shard.reshape(2, half, columns)
        near = lax.ppermute(pieces, both, role)
        if direct:
            far = lax.ppermute(one(pieces, c), both, across_chip)
        else:
            far = lax.ppermute(one(near, c), both, turn)
        near_other = lax.ppermute(near, "ctx", swap)
        far_other = lax.ppermute(far, "ctx", swap)
        return (
            shard, near.reshape(chunk, columns), near_other.reshape(chunk, columns), far[0], far_other[0]
        )

    def scatter_rows(keep, send):
        got = lax.ppermute(send, "ctx", swap)
        far = lax.ppermute(add(keep[2:3], got[2:3]), both, turn)
        which = iota((2, 1, 1), 0) == c
        near = add(keep[0:2], got[0:2], jnp.where(which, far.astype(F32), 0.0))
        near = lax.ppermute(near, both, role)
        other = lax.ppermute(one(near, 1 - c), "ctx", swap)
        own = keep[3].astype(F32) + got[3].astype(F32)
        return own + one(near, c)[0].astype(F32) + other[0].astype(F32)

    def scatter_tp(pieces):
        if not line:
            full = jnp.concatenate(pieces, axis=1)
            total = lax.psum_scatter(full, "tp", scatter_dimension=1, tiled=True)
            return total, jnp.zeros_like(total), jnp.zeros_like(total)
        right = left = None
        for r in range(1, nt):
            a, b = pieces[nt - r], pieces[r]
            if right is not None:
                a, b = add(a, right), add(b, left)
            right = lax.ppermute(a, "tp", [(i, i + 1) for i in range(r)])
            left = lax.ppermute(b, "tp", [(i, i - 1) for i in range(nt - r, nt)])
        return pieces[0], right, left

    any_spec = pl.BlockSpec(memory_space=pl.ANY)
    sems = pltpu.SemaphoreType.DMA((5,))

    def block(columns, back=False):
        if back:
            return pl.BlockSpec((STRETCH, columns), lambda i, *_: (nb - 1 - i, 0))
        return pl.BlockSpec((STRETCH, columns), lambda i, *_: (i, 0))

    def across(back=False):
        if back:
            return pl.BlockSpec((8, STRETCH), lambda i, *_: (0, nb - 1 - i))
        return pl.BlockSpec((8, STRETCH), lambda i, *_: (0, i))

    def stacked(rows, columns, back=False, off=0):
        if back:
            return pl.BlockSpec((1, rows, columns), lambda i, *_: (nb - 1 - i + off, 0, 0))
        return pl.BlockSpec((1, rows, columns), lambda i, *_: (i + off, 0, 0))

    def main_part(which):
        return pl.BlockSpec((1, chunk, channels), lambda i: (which, 0, 0))

    tokens2, cot2 = tokens[0], cotangent[0]
    ins = (proj_shared, proj_step, proj_main)
    outs = (shape((chunk, lead), BF),)
    shard_in = call(
        pack_in_kernel, (1,), ins, [whole(proj_shared), whole(proj_step), main_part(1)],
        outs, [whole(outs[0])],
    )[0]
    w_in = gather_rows(shard_in, False)
    halo = lax.ppermute(tokens2[length - HALO :], "ctx", [(0, 1)])
    ins = (proj_main, output_projection)
    outs = (shape((chunk, 2 * wide), BF),)
    shard_go = call(
        pack_go_kernel, (1,), ins, [main_part(0), whole(output_projection)],
        outs, [whole(outs[0])],
    )[0]
    w_go = gather_rows(shard_go, True)

    gate_row = gate_gain[None]
    gain_row = norm_gain[None]

    ins = (idx, tokens2, halo, cot2, gain_row, segments)
    outs = (
        shape((length, width), BF), shape((HALO, width), BF), shape((length, chunk), BF),
        shape((length, chunk), BF), shape((length, LANES), F32), shape((8, length), F32),
    )
    normed, nhalo, own_tokens, own_cot, inv_rms, tab = call(
        functools.partial(prep_kernel, chunk), (nb,), ins,
        [block(width), whole(halo), block(width), whole(gain_row), whole(segments)],
        outs, [block(width), whole(outs[1]), block(chunk), block(chunk), block(LANES), across()], prefetch=1,
    )
    if not line:
        own_tokens = lax.dynamic_slice_in_dim(tokens2, t * share, share, 1)
        own_cot = lax.dynamic_slice_in_dim(cot2, t * share, share, 1)

    outs = (
        shape((length, lead), BF), shape((HALO, lead), BF),
        shape((length, channels), BF), shape((length, channels), BF), shape((length, channels), BF),
        shape((length, SHARED), BF), shape((length, SHARED), BF),
        shape((length, LANES), F32), shape((length, LANES), F32), shape((length, LANES), F32),
        shape((nb, STATE, channels), F32), shape((nb, 8, channels), F32), shape((STATE, channels), BF),
    )
    ins = (idx, *w_in, normed, nhalo, conv_main, conv_shared, head_params, tab)
    wide_row = pltpu.VMEM((8, LANES), F32)
    held_in = pltpu.VMEM((nf, chunk, lead), BF)
    pre, phalo, x, xs, slope, bc, slopes, step, cum, sgm, states, fac, total = call(
        first_kernel, (nb,), ins,
        [any_spec] * 5
        + [block(width), whole(nhalo), whole(conv_main), whole(conv_shared), whole(head_params), across()],
        outs,
        [block(lead), whole(outs[1])] + [block(channels)] * 3 + [block(SHARED)] * 2 + [block(LANES)] * 3
        + [stacked(STATE, channels), stacked(8, channels), whole(outs[-1])],
        scratch=[
            held_in, sems, pltpu.VMEM((HALO, lead), BF), pltpu.VMEM((STATE, channels), F32), wide_row,
            pltpu.VMEM((channels, LANES), BF),
        ],
        prefetch=1, flops=2 * length * (STATE * channels + width * lead),
    )
    enter = lax.ppermute(total, "ctx", [(0, 1)])

    outs = (shape((length, channels), F32), shape((nb + 1, STATE, channels), BF))
    ins = (bc, x, xs, cum, states, fac, enter, head_params, tab)
    y, hist = call(
        second_kernel, (nb,), ins,
        [
            block(SHARED), block(channels), block(channels), block(LANES), stacked(STATE, channels),
            stacked(8, channels), whole(enter), whole(head_params), across(),
        ],
        outs, [block(channels), whole(outs[1])],
        scratch=[pltpu.VMEM((STATE, channels), F32), wide_row, pltpu.VMEM((8, channels), F32)],
        flops=8 * length * STRETCH * channels,
    )

    outs = (shape((length, channels), BF),) * 2 + (shape((length, chunk), BF),) * nf + (shape((8, length), F32),)
    ins = (idx, *w_go, normed, y, cot2, gate_row)
    gate, gg, *out_parts, stat = call(
        gate_kernel, (nb,), ins,
        [any_spec] * 5 + [block(width), block(channels), block(width), whole(gate_row)],
        outs, [block(channels)] * 2 + [block(chunk)] * nf + [across()],
        scratch=[pltpu.VMEM((nf, chunk, 2 * wide), BF), sems],
        prefetch=1, flops=4 * length * width * channels,
    )
    out_terms = scatter_tp(out_parts)
    stat = tp_sum(stat)
    outs = (shape((length, channels), BF),)
    gng = call(
        gng_kernel, (nb,), (idx, *w_go, cot2), [any_spec] * 5 + [block(width)], outs, [block(channels)],
        scratch=[pltpu.VMEM((nf, chunk, wide), BF), sems], prefetch=1, flops=2 * length * width * channels,
    )[0]

    outs = (
        shape((length, channels), BF), shape((length, channels), BF), shape((length, LANES), F32),
        shape((STATE, channels), BF), shape((8, channels), F32),
    )
    ins = (stat, y, gate, gng, gate_row, bc, cum, fac, tab)
    gy, gi, inv_gate, flow, gate_grad = call(
        third_kernel, (nb,), ins,
        [
            across(True), block(channels, True), block(channels, True), block(channels, True), whole(gate_row),
            block(SHARED, True), block(LANES, True), stacked(8, channels, True), across(True),
        ],
        outs, [block(channels, True), block(channels, True), block(LANES, True), whole(outs[3]), whole(outs[4])],
        scratch=[pltpu.VMEM((STATE, channels), F32)],
        flops=2 * length * STATE * channels,
    )
    leaving = lax.ppermute(flow, "ctx", [(1, 0)])

    outs = (shape((4, half, 2 * wide), BF),) * 2
    ins = (idx, normed, gi, cot2, inv_gate, gg)
    grad_go = call(
        gate_out_kernel, (nf,), ins,
        [
            pl.BlockSpec((length, chunk), lambda i, *_: (0, i)), whole(gi),
            pl.BlockSpec((length, chunk), lambda i, *_: (0, i)), whole(inv_gate), whole(gg),
        ],
        outs, [whole(outs[0])] * 2, prefetch=1,
        flops=4 * length * width * channels,
    )
    grad_go = scatter_rows(*grad_go)

    outs = (
        shape((length, lead), BF), shape((HALO, lead), BF), shape((16, width), F32), shape((HALO, width), F32),
    )
    ins = (
        idx, *w_in, gy, x, xs, slope, y, bc, slopes, step, cum, sgm, pre, pre, phalo, hist, hist, fac, leaving,
        conv_main, conv_shared, head_params, tab, gate_grad,
    )
    per_block = STRETCH // HALO
    g_in, ghalo, small, back = call(
        fourth_kernel, (nb,), ins,
        [any_spec] * 5
        + [block(channels, True)] * 5 + [block(SHARED, True)] * 2 + [block(LANES, True)] * 3
        + [
            block(lead, True),
            pl.BlockSpec((HALO, lead), lambda i, *_: (jnp.maximum((nb - 1 - i) * per_block - 1, 0), 0)),
            whole(phalo), stacked(STATE, channels, True), stacked(STATE, channels, True, 1),
            stacked(8, channels, True), whole(leaving), whole(conv_main), whole(conv_shared),
            whole(head_params), across(True), whole(gate_grad),
        ],
        outs, [block(lead, True)] + [whole(o) for o in outs[1:]],
        scratch=[
            held_in, sems, pltpu.VMEM((STATE, channels), F32), pltpu.VMEM((HALO, lead), F32), wide_row,
            pltpu.VMEM((channels, LANES), BF), pltpu.VMEM((8, channels), F32), pltpu.VMEM((8, channels), F32),
            pltpu.VMEM((8, channels), F32), pltpu.VMEM((8, SHARED), F32), wide_row,
        ],
        prefetch=1, flops=16 * length * STRETCH * channels,
    )
    back = lax.ppermute(back, "ctx", [(1, 0)])

    outs = (shape((length, chunk), BF),) * nf + (shape((8, length), F32), shape((16, width), F32))
    ins = (idx, *w_go, *w_in, gi, g_in, normed, back, small)
    *normed_parts, cross, sums = call(
        normed_kernel, (nb,), ins,
        [any_spec] * 10 + [block(channels), block(lead), block(width), whole(back), whole(small)],
        outs, [block(chunk)] * nf + [across(), whole(outs[-1])],
        scratch=[
            pltpu.VMEM((nf, chunk, wide), BF), held_in, sems, sems, pltpu.VMEM((STRETCH, chunk), F32),
        ],
        prefetch=1, flops=2 * length * width * (lead + channels),
    )
    normed_terms = scatter_tp(normed_parts)
    cross = tp_sum(cross)

    outs = (shape((4, half, lead), BF),) * 2
    grad_w = call(
        weight_kernel, (nf,), (idx, normed, nhalo, g_in, ghalo),
        [
            pl.BlockSpec((length, chunk), lambda i, *_: (0, i)), pl.BlockSpec((HALO, chunk), lambda i, *_: (0, i)),
            whole(g_in), whole(ghalo),
        ],
        outs, [whole(outs[0])] * 2, prefetch=1,
        flops=2 * length * width * lead,
    )
    grad_w = scatter_rows(*grad_w)

    sums = sums + lax.ppermute(sums, "ctx", swap)
    for m in (1, 2):
        sums = sums + lax.ppermute(sums, "fsdp", [(i, i ^ m) for i in range(nf)])
    over_tp = tp_sum(sums)
    own_gain = lax.dynamic_slice_in_dim(norm_gain, t * share, share, 0)
    grad_gain = lax.dynamic_slice_in_dim(over_tp[0], t * share, share, 0) / own_gain

    outs = (shape((length, share), BF),)
    if line:
        spec = pl.BlockSpec((length // 2, share), lambda i: (i, 0))
        inv_spec = pl.BlockSpec((length // 2, LANES), lambda i: (i, 0))
        output = call(
            output_kernel, (2,), (own_tokens, inv_gate, *out_terms), [spec, inv_spec, spec, spec, spec],
            outs, [spec],
        )[0]
        outs = (shape((length, share), F32),)
        gain2 = own_gain[None]
        grad_tokens = call(
            functools.partial(tokens_kernel, width), (2,),
            (own_tokens, own_cot, inv_rms, cross, gain2, *normed_terms),
            [
                spec, spec, inv_spec, pl.BlockSpec((8, length // 2), lambda i: (0, i)), whole(gain2), spec, spec,
                spec,
            ],
            outs, [spec],
        )[0]
    else:
        output = (own_tokens.astype(F32) + inv_gate[:, :1] * out_terms[0].astype(F32)).astype(BF)
        inv = inv_rms[:, :1]
        grad_tokens = (
            inv * own_gain * normed_terms[0].astype(F32)
            - own_tokens.astype(F32) * (inv * inv * (cross[0][:, None] / width))
            + own_cot.astype(F32)
        )
    return (
        output[None],
        grad_tokens[None],
        grad_gain,
        jnp.stack([grad_go[:, :channels], grad_w[:, LEAD:]]),
        tp_sum(grad_w[:, :SHARED]),
        grad_w[:, SHARED : SHARED + heads],
        sums[1:6, :channels],
        over_tp[6:11, :SHARED],
        sums[12:15, :heads],
        sums[11, :channels],
        jnp.transpose(grad_go[:, wide : wide + channels]),
    )


def solution(mesh):
    return jax.shard_map(
        per_device,
        mesh=mesh,
        in_specs=(
            P("fsdp", "ctx", None),
            P("fsdp", None),
            P(),
            P(None, "fsdp", "tp"),
            P("fsdp", None),
            P("fsdp", "tp"),
            P(None, "tp"),
            P(),
            P(None, "tp"),
            P("tp"),
            P("tp", "fsdp"),
            P("fsdp", "ctx", None),
        ),
        out_specs=(
            P("fsdp", "ctx", "tp"),
            P("fsdp", "ctx", "tp"),
            P("tp"),
            P(None, ("fsdp", "ctx"), "tp"),
            P(("fsdp", "ctx"), None),
            P(("fsdp", "ctx"), "tp"),
            P(None, "tp"),
            P(),
            P(None, "tp"),
            P("tp"),
            P("tp", ("fsdp", "ctx")),
        ),
        check_vma=False,
    )
```

profile of v0, /device:TPU:0, one launch (start us, length us, event | category | flops | bytes accessed | tf_op | source)
XLA Modules:
  0.0 361.1 jit_solution(15580213084130575429)
XLA Ops:
  9.9 8.7 %collective-permute-done.5 = bf16[2,192,1152]{2,1,0:T(8,128)(2,1)S(1)} collective-permute-done((bf16[2,192,1152]{2,1,0:T(8,128)(2,1)}, bf16[2,192,1152]{2,1,0:T(8,128)(2,1)S(1)}, u32[]{:S(2)}, u32[]{:S(2)}) %collective-permute-start.5) | collective-permute-done | bytes 884768 | tf_op jit(solution)/shard_map/ppermute | solution.py:770
  24.1 17.8 %collective-permute-done.1 = bf16[2,192,1536]{2,1,0:T(8,128)(2,1)S(1)} collective-permute-done((bf16[2,192,1536]{2,1,0:T(8,128)(2,1)}, bf16[2,192,1536]{2,1,0:T(8,128)(2,1)S(1)}, u32[]{:S(2)}, u32[]{:S(2)}) %collective-permute-start.1) | collective-permute-done | bytes 1179680 | tf_op jit(solution)/shard_map/ppermute | solution.py:770
  47.0 6.8 %shard_map.203 = (bf16[1024,1536]{1,0:T(8,128)(2,1)}, bf16[16,1536]{1,0:T(8,128)(2,1)}, bf16[1024,384]{1,0:T(8,128)(2,1)}, bf16[1024,384]{1,0:T(8,128)(2,1)}, f32[1024,128]{1,0:T(8,128)}, /*index=5*/f32[8,1024]{1,0:T(8,128)}) custom-call(s32[8]{0:T(128)} %stack.38.idx_ref, bf16[1024,1536]{1,0:T(8,128)(2,1)} %bitcast.45, bf16[16,1536]{1,0:T(8,128)(2,1)} %copy-done.18, ...), custom_call_target="tpu_custom_call" | custom-call | bytes 11679776 | tf_op jit(solution)/shard_map/pallas_call | solution.py:703
  54.0 20.0 %shard_map.206 = (bf16[1024,1152]{1,0:T(8,128)(2,1)}, bf16[16,1152]{1,0:T(8,128)(2,1)}, bf16[1024,768]{1,0:T(8,128)(2,1)}, bf16[1024,768]{1,0:T(8,128)(2,1)}, bf...) custom-call(s32[8]{0:T(128)} %stack.38.idx_ref, ...), custom_call_target="tpu_custom_call" | custom-call | flops 3825205248 | bytes 18391216 | tf_op jit(solution)/shard_map/pallas_call | solution.py:703
  78.3 9.1 %shard_map.207 = (f32[1024,768]{1,0:T(8,128)}, bf16[5,128,768]{2,1,0:T(8,128)(2,1)}) custom-call(bf16[1024,256]{1,0:T(8,128)(2,1)} %get-tuple-element.62.bc_ref, bf16[1024,768]{1,0:T(8,128)(2,1)} %get-tuple-element.63.x_ref, bf16[1024,768]{1,0:T(8,128)(2,1)} %get-tuple-element.64.xs_ref, f32[1024,128]{1,0:T(8,128)} %get-tuple-element.65.cum_ref, ...), custom_call_target="tpu_custom_call" | custom-call | flops 1610612736 | bytes 10223760 | tf_op jit(solution)/shard_map/pallas_call | solution.py:703
  88.5 16.2 %shard_map.208 = (bf16[1024,768]{1,0:T(8,128)(2,1)}, bf16[1024,768]{1,0:T(8,128)(2,1)}, bf16[1024,384]{1,0:T(8,128)(2,1)}, bf16[1024,384]{1,0:T(8,128)(2,1)}, bf...) custom-call(s32[8]{0:T(128)} %stack.38.idx_ref, ...), custom_call_target="tpu_custom_call" | custom-call | flops 4831838208 | bytes 20483104 | tf_op jit(solution)/shard_map/pallas_call | solution.py:703
  109.8 8.5 %shard_map.209.gng_ref = bf16[1024,768]{1,0:T(8,128)(2,1)} custom-call(s32[8]{0:T(128)} %stack.38.idx_ref, bf16[384,1536]{1,0:T(8,128)(2,1)} %shard_map.204.own_ref.own0_ref, bf16[384,1536]{1,0:T(8,128)(2,1)} %bitcast.51, bf16[384,1536]{1,0:T(8,128)(2,1)} %bitcast.54, bf16[192,1536]{1,0:T(8,128)(2,1)} %bitcast.12.far_ref.far0_ref, ...), custom_call_target="tpu_custom_call" | custom-call | flops 2415919104 | bytes 9437216 | tf_op jit(solution)/shard_map/pallas_call | solution.py:703
  119.0 8.5 %shard_map.210 = (bf16[1024,768]{1,0:T(8,128)(2,1)}, bf16[1024,768]{1,0:T(8,128)(2,1)}, f32[1024,128]{1,0:T(8,128)}, bf16[128,768]{1,0:T(8,128)(2,1)}, f32[8,768]{1,0:T(8,128)}) custom-call(f32[8,1024]{1,0:T(8,128)} %add_add_fusion.3.stat_ref, f32[1024,768]{1,0:T(8,128)} %get-tuple-element.69.y_ref, bf16[1024,768]{1,0:T(8,128)(2,1)} %get-tuple-element.71.gate_ref, ...), custom_call_target="tpu_custom_call" | custom-call | flops 201326592 | bytes 11398144 | tf_op jit(solution)/shard_map/pallas_call | solution.py:703
  131.7 23.6 %shard_map.212 = (bf16[1024,1152]{1,0:T(8,128)(2,1)}, bf16[16,1152]{1,0:T(8,128)(2,1)}, f32[16,1536]{1,0:T(8,128)}, f32[16,1536]{1,0:T(8,128)}) custom-call(s32[8]{0:T(128)} %stack.38.idx_ref, bf16[384,1152]{1,0:T(8,128)(2,1)} %shard_map.205.own_ref, bf16[384,1152]{1,0:T(8,128)(2,1)} %bitcast.47, bf16[384,1152]{1,0:T(8,128)(2,1)} %bitcast.16.nearx_ref, ...), custom_call_target="tpu_custom_call" | custom-call | flops 3221225472 | bytes 25284784 | tf_op jit(solution)/shard_map/pallas_call | solution.py:703
  159.4 18.7 %shard_map.213 = (bf16[1024,384]{1,0:T(8,128)(2,1)}, bf16[1024,384]{1,0:T(8,128)(2,1)}, bf16[1024,384]{1,0:T(8,128)(2,1)}, bf16[1024,384]{1,0:T(8,128)(2,1)}, f32[8,1024]{1,0:T(8,128)}, /*index=5*/f32[16,1536]{1,0:T(8,128)}) custom-call(s32[8]{0:T(128)} %stack.38.idx_ref, bf16[384,1536]{1,0:T(8,128)(2,1)} %shard_map.204.own_ref.own0_ref, ...), custom_call_target="tpu_custom_call" | custom-call | flops 6039797760 | bytes 18808864 | tf_op jit(solution)/shard_map/pallas_call | solution.py:703
  190.1 14.4 %shard_map.215 = (bf16[4,192,1536]{2,1,0:T(8,128)(2,1)}, bf16[4,192,1536]{2,1,0:T(8,128)(2,1)}) custom-call(s32[8]{0:T(128)} %stack.38.idx_ref, bf16[1024,1536]{1,0:T(8,128)(2,1)} %get-tuple-element.59.normed_ref, bf16[1024,768]{1,0:T(8,128)(2,1)} %get-tuple-element.79.gi_ref, bf16[1024,1536]{1,0:T(8,128)(2,1)} %bitcast.41, ...), custom_call_target="tpu_custom_call" | custom-call | flops 4831838208 | bytes 14680096 | tf_op jit(solution)/shard_map/pallas_call | solution.py:703
  205.9 10.9 %shard_map.216 = (bf16[4,192,1152]{2,1,0:T(8,128)(2,1)}, bf16[4,192,1152]{2,1,0:T(8,128)(2,1)}) custom-call(s32[8]{0:T(128)} %stack.38.idx_ref, bf16[1024,1536]{1,0:T(8,128)(2,1)} %get-tuple-element.59.normed_ref, bf16[16,1536]{1,0:T(8,128)(2,1)} %get-tuple-element.60.nhalo_ref, bf16[1024,1152]{1,0:T(8,128)(2,1)} %get-tuple-element.90.g_ref, ...), custom_call_target="tpu_custom_call" | custom-call | flops 3623878656 | bytes 9130016 | tf_op jit(solution)/shard_map/pallas_call | solution.py:703
  216.8 4.7 %collective-permute-done.23 = f32[8,1024]{1,0:T(8,128)S(1)} collective-permute-done((f32[8,1024]{1,0:T(8,128)S(1)}, f32[8,1024]{1,0:T(8,128)S(1)}, u32[]{:S(2)}, u32[]{:S(2)}) %collective-permute-start.23) | collective-permute-done | bytes 32800 | tf_op jit(solution)/shard_map/ppermute | solution.py:760
  235.4 6.7 %collective-permute-start.33 = (f32[16,1536]{1,0:T(8,128)S(1)}, f32[16,1536]{1,0:T(8,128)S(1)}, u32[]{:S(2)}, u32[]{:S(2)}) collective-permute-start(f32[16,1536]{1,0:T(8,128)S(1)} %add.152), channel_id=1, source_target_pairs={{0,1},{1,0},{2,3},{3,2},{4,5},{5,4},{6,7},{7,6},{8,9},{9,8},{10,11... | collective-permute-start | bytes 294920 | tf_op jit(solution)/shard_map/ppermute | solution.py:760
  242.3 6.3 %collective-permute-done.14 = bf16[1024,384]{1,0:T(8,128)(2,1)S(1)} collective-permute-done((bf16[1024,384]{1,0:T(8,128)(2,1)}, bf16[1024,384]{1,0:T(8,128)(2,1)S(1)}, u32[]{:S(2)}, u32[]{:S(2)}) %collective-permute-start.14) | collective-permute-done | bytes 786464 | tf_op jit(solution)/shard_map/ppermute | solution.py:801
  249.4 15.3 %collective-permute-start.35 = (f32[16,1536]{1,0:T(8,128)S(1)}, f32[16,1536]{1,0:T(8,128)S(1)}, u32[]{:S(2)}, u32[]{:S(2)}) collective-permute-start(f32[16,1536]{1,0:T(8,128)S(1)} %add.152), channel_id=1, source_target_pairs={{0,3},{1,2},{2,1},{3,0},{4,7},{5,6},{6,5},{7,4},{8,11},{9,10},{10,... | collective-permute-start | bytes 294920 | tf_op jit(solution)/shard_map/ppermute | solution.py:760
  273.4 5.6 %collective-permute-done.41 = bf16[1,192,1152]{2,1,0:T(8,128)(2,1)S(1)} collective-permute-done((bf16[1,192,1152]{2,1,0:T(8,128)(2,1)S(1)}, bf16[1,192,1152]{2,1,0:T(8,128)(2,1)S(1)}, u32[]{:S(2)}, u32[]{:S(2)}) %collective-permute-start.41) | collective-permute-done | bytes 442400 | tf_op jit(solution)/shard_map/ppermute | solution.py:783
  282.1 8.8 %collective-permute-done.37 = bf16[1,192,1536]{2,1,0:T(8,128)(2,1)S(1)} collective-permute-done((bf16[1,192,1536]{2,1,0:T(8,128)(2,1)S(1)}, bf16[1,192,1536]{2,1,0:T(8,128)(2,1)S(1)}, u32[]{:S(2)}, u32[]{:S(2)}) %collective-permute-start.37) | collective-permute-done | bytes 589856 | tf_op jit(solution)/shard_map/ppermute | solution.py:783
  297.4 4.6 %collective-permute-start.15 = (bf16[1024,384]{1,0:T(8,128)(2,1)S(1)}, bf16[1024,384]{1,0:T(8,128)(2,1)S(1)}, u32[]{:S(2)}, u32[]{:S(2)}) collective-permute-start(bf16[1024,384]{1,0:T(8,128)(2,1)S(1)} %add_convert_fusion.5), channel_id=1, source_target_pairs={{0,1},{1,2},{2,3},{4,5},{5,6},{6,7},{8,9},{9,10},{10,11},{12,13},{... | collective-permute-start | bytes 2359304 | tf_op jit(solution)/shard_map/ppermute | solution.py:801
  303.9 4.9 %collective-permute-start.26 = (bf16[1024,384]{1,0:T(8,128)(2,1)}, bf16[1024,384]{1,0:T(8,128)(2,1)}, u32[]{:S(2)}, u32[]{:S(2)}) collective-permute-start(bf16[1024,384]{1,0:T(8,128)(2,1)} %add_convert_fusion.3), channel_id=1, source_target_pairs={{0,1},{1,2},{2,3},{4,5},{5,6},{6,7},{8,9},{9,10},{10,11},{12,13},{... | collective-permute-start | bytes 2359304 | tf_op jit(solution)/shard_map/ppermute | solution.py:801
  309.6 7.6 %collective-permute-done.18.left_ref = bf16[1024,384]{1,0:T(8,128)(2,1)S(1)} collective-permute-done((bf16[1024,384]{1,0:T(8,128)(2,1)S(1)}, bf16[1024,384]{1,0:T(8,128)(2,1)S(1)}, u32[]{:S(2)}, u32[]{:S(2)}) %collective-permute-start.18) | collective-permute-done | bytes 786464 | tf_op jit(solution)/shard_map/ppermute | solution.py:802
  328.4 3.7 %shard_map.214 = f32[1024,384]{1,0:T(8,128)} custom-call(bf16[1024,384]{1,0:T(8,128)(2,1)} %get-tuple-element.58.own_ref, bf16[1024,384]{1,0:T(8,128)(2,1)} %get-tuple-element.77.cot_ref, f32[1024,128]{1,0:T(8,128)} %get-tuple-element.78.inv_ref, f32[8,1024]{1,0:T(8,128)} %add_add_fusion.2.cross_ref, f32[1,384]{1,0:T(1,128)} %broadcast_in_dim.68.gain_ref, ...), custom_call_target="tpu_custom_call" | custom-call | bytes 6063616 | tf_op jit(solution)/shard_map/pallas_call | solution.py:703
  341.5 5.3 %collective-permute-done.44 = f32[192,256]{1,0:T(8,128)} collective-permute-done((f32[192,256]{1,0:T(8,128)S(1)}, f32[192,256]{1,0:T(8,128)}, u32[]{:S(2)}, u32[]{:S(2)}) %collective-permute-start.44) | collective-permute-done | bytes 196640 | tf_op jit(solution)/shard_map/ppermute | solution.py:760
  346.8 8.8 %collective-permute-done.45 = f32[192,256]{1,0:T(8,128)} collective-permute-done((f32[192,256]{1,0:T(8,128)S(1)}, f32[192,256]{1,0:T(8,128)}, u32[]{:S(2)}, u32[]{:S(2)}) %collective-permute-start.45) | collective-permute-done | bytes 196640 | tf_op jit(solution)/shard_map/ppermute | solution.py:760
  (177 shorter events, 114.4 us)
Async XLA Ops:
  9.9 32.0 %collective-permute-start.1 = (bf16[2,192,1536]{2,1,0:T(8,128)(2,1)}, bf16[2,192,1536]{2,1,0:T(8,128)(2,1)S(1)}, u32[]{:S(2)}, u32[]{:S(2)}) collective-permute-start(bf16[2,192,1536]{2,1,0:T(8,128)(2,1)} %bitcast.42), channel_id=1, source_target_pairs={{0,8},{4,20},{8,0},{12,28},{16,24},{20,4},{24,16},{28,12},{1,9},{5... | collective-permute-start | bytes 3538952 | tf_op jit(solution)/shard_map/ppermute | solution.py:770
  18.6 23.3 %collective-permute-start.7 = (bf16[1,192,1152]{2,1,0:T(8,128)(2,1)S(1)}, bf16[1,192,1152]{2,1,0:T(8,128)(2,1)}, u32[]{:S(2)}, u32[]{:S(2)}) collective-permute-start(bf16[1,192,1152]{2,1,0:T(8,128)(2,1)S(1)} %constant_dynamic-slice_fusion.3), channel_id=1, source_target_pairs={{0,16},{4,12},{8,24},{12,4},{16,0},{20,28},{24,8},{28,20},{1,17},{... | collective-permute-start | bytes 1327112 | tf_op jit(solution)/shard_map/ppermute | solution.py:774
  20.7 33.2 %collective-permute-start.6 = (bf16[2,192,1152]{2,1,0:T(8,128)(2,1)S(1)}, bf16[2,192,1152]{2,1,0:T(8,128)(2,1)}, u32[]{:S(2)}, u32[]{:S(2)}) collective-permute-start(bf16[2,192,1152]{2,1,0:T(8,128)(2,1)S(1)} %collective-permute-done.5), channel_id=1, source_target_pairs={{0,4},{4,0},{1,5},{5,1},{2,6},{6,2},{3,7},{7,3},{8,12},{12,8},{9,1... | collective-permute-start | bytes 2654216 | tf_op jit(solution)/shard_map/ppermute | solution.py:775
  22.7 31.2 %collective-permute-start.3 = (bf16[1,192,1536]{2,1,0:T(8,128)(2,1)}, bf16[1,192,1536]{2,1,0:T(8,128)(2,1)}, u32[]{:S(2)}, u32[]{:S(2)}) collective-permute-start(bf16[1,192,1536]{2,1,0:T(8,128)(2,1)} %constant_dynamic-slice_fusion.4), channel_id=1, source_target_pairs={{0,24},{4,28},{8,16},{12,20},{16,8},{20,12},{24,0},{28,4},{1,25},{... | collective-permute-start | bytes 1769480 | tf_op jit(solution)/shard_map/ppermute | solution.py:772
  41.9 45.5 %collective-permute-start.2 = (bf16[2,192,1536]{2,1,0:T(8,128)(2,1)S(1)}, bf16[2,192,1536]{2,1,0:T(8,128)(2,1)S(1)}, u32[]{:S(2)}, u32[]{:S(2)}) collective-permute-start(bf16[2,192,1536]{2,1,0:T(8,128)(2,1)S(1)} %collective-permute-done.1), channel_id=1, source_target_pairs={{0,4},{4,0},{1,5},{5,1},{2,6},{6,2},{3,7},{7,3},{8,12},{12,8},{9,1... | collective-permute-start | bytes 3538952 | tf_op jit(solution)/shard_map/ppermute | solution.py:775
  53.9 33.5 %collective-permute-start.4 = (bf16[1,192,1536]{2,1,0:T(8,128)(2,1)}, bf16[1,192,1536]{2,1,0:T(8,128)(2,1)}, u32[]{:S(2)}, u32[]{:S(2)}) collective-permute-start(bf16[1,192,1536]{2,1,0:T(8,128)(2,1)} %collective-permute-done.3), channel_id=1, source_target_pairs={{0,4},{4,0},{1,5},{5,1},{2,6},{6,2},{3,7},{7,3},{8,12},{12,8},{9,1... | collective-permute-start | bytes 1769480 | tf_op jit(solution)/shard_map/ppermute | solution.py:776
  182.6 38.9 %collective-permute-start.13 = (bf16[1024,384]{1,0:T(8,128)(2,1)S(1)}, bf16[1024,384]{1,0:T(8,128)(2,1)S(1)}, u32[]{:S(2)}, u32[]{:S(2)}) collective-permute-start(bf16[1024,384]{1,0:T(8,128)(2,1)S(1)} %copy-done.8), channel_id=1, source_target_pairs={{0,1},{4,5},{8,9},{12,13},{16,17},{20,21},{24,25},{28,29}} | collective-permute-start | bytes 2359304 | tf_op jit(solution)/shard_map/ppermute | solution.py:801
  184.6 37.4 %collective-permute-start.16 = (bf16[1024,384]{1,0:T(8,128)(2,1)S(1)}, bf16[1024,384]{1,0:T(8,128)(2,1)}, u32[]{:S(2)}, u32[]{:S(2)}) collective-permute-start(bf16[1024,384]{1,0:T(8,128)(2,1)S(1)} %copy-done.6), channel_id=1, source_target_pairs={{3,2},{7,6},{11,10},{15,14},{19,18},{23,22},{27,26},{31,30}} | collective-permute-start | bytes 2359304 | tf_op jit(solution)/shard_map/ppermute | solution.py:802
  186.2 41.4 %collective-permute-start.24 = (bf16[1024,384]{1,0:T(8,128)(2,1)}, bf16[1024,384]{1,0:T(8,128)(2,1)}, u32[]{:S(2)}, u32[]{:S(2)}) collective-permute-start(bf16[1024,384]{1,0:T(8,128)(2,1)} %get-tuple-element.97), channel_id=1, source_target_pairs={{0,1},{4,5},{8,9},{12,13},{16,17},{20,21},{24,25},{28,29}} | collective-permute-start | bytes 2359304 | tf_op jit(solution)/shard_map/ppermute | solution.py:801
  188.4 40.7 %collective-permute-start.27 = (bf16[1024,384]{1,0:T(8,128)(2,1)}, bf16[1024,384]{1,0:T(8,128)(2,1)}, u32[]{:S(2)}, u32[]{:S(2)}) collective-permute-start(bf16[1024,384]{1,0:T(8,128)(2,1)} %get-tuple-element.95), channel_id=1, source_target_pairs={{3,2},{7,6},{11,10},{15,14},{19,18},{23,22},{27,26},{31,30}} | collective-permute-start | bytes 2359304 | tf_op jit(solution)/shard_map/ppermute | solution.py:802
  221.5 49.1 %collective-permute-start.36 = (bf16[4,192,1536]{2,1,0:T(8,128)(2,1)}, bf16[4,192,1536]{2,1,0:T(8,128)(2,1)}, u32[]{:S(2)}, u32[]{:S(2)}) collective-permute-start(bf16[4,192,1536]{2,1,0:T(8,128)(2,1)} %get-tuple-element.101), channel_id=1, source_target_pairs={{0,4},{4,0},{1,5},{5,1},{2,6},{6,2},{3,7},{7,3},{8,12},{12,8},{9,1... | collective-permute-start | bytes 7077896 | tf_op jit(solution)/shard_map/ppermute | solution.py:782
  221.5 44.4 %collective-permute-start.40 = (bf16[4,192,1152]{2,1,0:T(8,128)(2,1)}, bf16[4,192,1152]{2,1,0:T(8,128)(2,1)}, u32[]{:S(2)}, u32[]{:S(2)}) collective-permute-start(bf16[4,192,1152]{2,1,0:T(8,128)(2,1)} %get-tuple-element.104), channel_id=1, source_target_pairs={{0,4},{4,0},{1,5},{5,1},{2,6},{6,2},{3,7},{7,3},{8,12},{12,8},{9,1... | collective-permute-start | bytes 5308424 | tf_op jit(solution)/shard_map/ppermute | solution.py:782
  229.1 19.5 %collective-permute-start.14 = (bf16[1024,384]{1,0:T(8,128)(2,1)}, bf16[1024,384]{1,0:T(8,128)(2,1)S(1)}, u32[]{:S(2)}, u32[]{:S(2)}) collective-permute-start(bf16[1024,384]{1,0:T(8,128)(2,1)} %get-tuple-element.123), channel_id=1, source_target_pairs={{0,1},{1,2},{4,5},{5,6},{8,9},{9,10},{12,13},{13,14},{16,17},{17,1... | collective-permute-start | bytes 2359304 | tf_op jit(solution)/shard_map/ppermute | solution.py:801
  235.4 59.4 %collective-permute-start.33 = (f32[16,1536]{1,0:T(8,128)S(1)}, f32[16,1536]{1,0:T(8,128)S(1)}, u32[]{:S(2)}, u32[]{:S(2)}) collective-permute-start(f32[16,1536]{1,0:T(8,128)S(1)} %add.152), channel_id=1, source_target_pairs={{0,1},{1,0},{2,3},{3,2},{4,5},{5,4},{6,7},{7,6},{8,9},{9,8},{10,11... | collective-permute-start | bytes 294920 | tf_op jit(solution)/shard_map/ppermute | solution.py:760
  248.7 48.8 %collective-permute-start.34 = (f32[16,1536]{1,0:T(8,128)S(1)}, f32[16,1536]{1,0:T(8,128)S(1)}, u32[]{:S(2)}, u32[]{:S(2)}) collective-permute-start(f32[16,1536]{1,0:T(8,128)S(1)} %add.152), channel_id=1, source_target_pairs={{0,2},{1,3},{2,0},{3,1},{4,6},{5,7},{6,4},{7,5},{8,10},{9,11},{10,... | collective-permute-start | bytes 294920 | tf_op jit(solution)/shard_map/ppermute | solution.py:760
  249.4 52.6 %collective-permute-start.35 = (f32[16,1536]{1,0:T(8,128)S(1)}, f32[16,1536]{1,0:T(8,128)S(1)}, u32[]{:S(2)}, u32[]{:S(2)}) collective-permute-start(f32[16,1536]{1,0:T(8,128)S(1)} %add.152), channel_id=1, source_target_pairs={{0,3},{1,2},{2,1},{3,0},{4,7},{5,6},{6,5},{7,4},{8,11},{9,10},{10,... | collective-permute-start | bytes 294920 | tf_op jit(solution)/shard_map/ppermute | solution.py:760
  265.9 30.2 %collective-permute-start.25 = (bf16[1024,384]{1,0:T(8,128)(2,1)S(1)}, bf16[1024,384]{1,0:T(8,128)(2,1)S(1)}, u32[]{:S(2)}, u32[]{:S(2)}) collective-permute-start(bf16[1024,384]{1,0:T(8,128)(2,1)S(1)} %get-tuple-element.121), channel_id=1, source_target_pairs={{0,1},{1,2},{4,5},{5,6},{8,9},{9,10},{12,13},{13,14},{16,17},{17,1... | collective-permute-start | bytes 2359304 | tf_op jit(solution)/shard_map/ppermute | solution.py:801
  294.8 22.3 %collective-permute-start.18 = (bf16[1024,384]{1,0:T(8,128)(2,1)S(1)}, bf16[1024,384]{1,0:T(8,128)(2,1)S(1)}, u32[]{:S(2)}, u32[]{:S(2)}) collective-permute-start(bf16[1024,384]{1,0:T(8,128)(2,1)S(1)} %add_convert_fusion.4), channel_id=1, source_target_pairs={{1,0},{2,1},{3,2},{5,4},{6,5},{7,6},{9,8},{10,9},{11,10},{13,12},{... | collective-permute-start | bytes 2359304 | tf_op jit(solution)/shard_map/ppermute | solution.py:802
  296.1 36.0 %collective-permute-start.38 = (bf16[2,192,1536]{2,1,0:T(8,128)(2,1)S(1)}, bf16[2,192,1536]{2,1,0:T(8,128)(2,1)}, u32[]{:S(2)}, u32[]{:S(2)}) collective-permute-start(bf16[2,192,1536]{2,1,0:T(8,128)(2,1)S(1)} %add_convert_fusion), channel_id=1, source_target_pairs={{0,8},{4,20},{8,0},{12,28},{16,24},{20,4},{24,16},{28,12},{1,9},{5... | collective-permute-start | bytes 3538952 | tf_op jit(solution)/shard_map/ppermute | solution.py:786
  297.4 22.5 %collective-permute-start.15 = (bf16[1024,384]{1,0:T(8,128)(2,1)S(1)}, bf16[1024,384]{1,0:T(8,128)(2,1)S(1)}, u32[]{:S(2)}, u32[]{:S(2)}) collective-permute-start(bf16[1024,384]{1,0:T(8,128)(2,1)S(1)} %add_convert_fusion.5), channel_id=1, source_target_pairs={{0,1},{1,2},{2,3},{4,5},{5,6},{6,7},{8,9},{9,10},{10,11},{12,13},{... | collective-permute-start | bytes 2359304 | tf_op jit(solution)/shard_map/ppermute | solution.py:801
  302.1 23.8 %collective-permute-start.29 = (bf16[1024,384]{1,0:T(8,128)(2,1)}, bf16[1024,384]{1,0:T(8,128)(2,1)}, u32[]{:S(2)}, u32[]{:S(2)}) collective-permute-start(bf16[1024,384]{1,0:T(8,128)(2,1)} %add_convert_fusion.2), channel_id=1, source_target_pairs={{1,0},{2,1},{3,2},{5,4},{6,5},{7,6},{9,8},{10,9},{11,10},{13,12},{... | collective-permute-start | bytes 2359304 | tf_op jit(solution)/shard_map/ppermute | solution.py:802
  303.9 24.5 %collective-permute-start.26 = (bf16[1024,384]{1,0:T(8,128)(2,1)}, bf16[1024,384]{1,0:T(8,128)(2,1)}, u32[]{:S(2)}, u32[]{:S(2)}) collective-permute-start(bf16[1024,384]{1,0:T(8,128)(2,1)} %add_convert_fusion.3), channel_id=1, source_target_pairs={{0,1},{1,2},{2,3},{4,5},{5,6},{6,7},{8,9},{9,10},{10,11},{12,13},{... | collective-permute-start | bytes 2359304 | tf_op jit(solution)/shard_map/ppermute | solution.py:801
  334.1 23.3 %collective-permute-start.39 = (bf16[1,192,1536]{2,1,0:T(8,128)(2,1)}, bf16[1,192,1536]{2,1,0:T(8,128)(2,1)}, u32[]{:S(2)}, u32[]{:S(2)}) collective-permute-start(bf16[1,192,1536]{2,1,0:T(8,128)(2,1)} %constant_dynamic-slice_fusion.1), channel_id=1, source_target_pairs={{0,4},{4,0},{1,5},{5,1},{2,6},{6,2},{3,7},{7,3},{8,12},{12,8},{9,1... | collective-permute-start | bytes 1769480 | tf_op jit(solution)/shard_map/ppermute | solution.py:787
  338.3 17.2 %collective-permute-start.45 = (f32[192,256]{1,0:T(8,128)S(1)}, f32[192,256]{1,0:T(8,128)}, u32[]{:S(2)}, u32[]{:S(2)}) collective-permute-start(f32[192,256]{1,0:T(8,128)S(1)} %slice.105), channel_id=1, source_target_pairs={{0,2},{1,3},{2,0},{3,1},{4,6},{5,7},{6,4},{7,5},{8,10},{9,11},{10,... | collective-permute-start | bytes 589832 | tf_op jit(solution)/shard_map/ppermute | solution.py:760
  (47 other events, 540.4 us)
where the time goes:
time: 364 us; the launch traced here: 361 us
  Pallas kernels  148 us (41%)
  starting transfers between devices  87.4 us (24%)
  waiting for transfers between devices  85.5 us (23%)
  other arithmetic  21.6 us (6%)
  local copies, waits for them, and re-layouts  17.2 us (5%)
    pallas_call x14, Pallas kernels, call(): pl.pallas_call(kernel, out_shape=outs, grid_spec=pltpu.PrefetchScalarGrid...  148 us
    ppermute x12, starting transfers between devices, tp_sum(): lax.ppermute(v, 'tp', [(i, i ^ m) for i in range(nt)])  38.6 us
    ppermute x2, waiting for transfers between devices, gather_rows(): near = lax.ppermute(pieces, both, role)  26.5 us
    ppermute x12, waiting for transfers between devices, tp_sum(): lax.ppermute(v, 'tp', [(i, i ^ m) for i in range(nt)])  18.8 us
    ppermute x6, starting transfers between devices, scatter_tp(): right = lax.ppermute(a, 'tp', [(i, i + 1) for i in range(r)])  18.7 us
    ppermute x2, waiting for transfers between devices, scatter_rows(): far = lax.ppermute(add(keep[2:3], got[2:3]), both, turn)  14.4 us
    convert_element_type x10, other arithmetic, add(): return sum((term.astype(F32) for term in terms)).astype(BF)  13.1 us
    ppermute x6, waiting for transfers between devices, scatter_tp(): right = lax.ppermute(a, 'tp', [(i, i + 1) for i in range(r)])  10.4 us
  transfers between devices with their start and end apart: 47, of which 17 were waited for; matrix products, arithmetic and copies ran while one was open for 8% of the time, Pallas kernels for 22%

commit v1 on v0

--- a/solution.py
+++ b/solution.py
@@ -20,7 +20,7 @@
 LEAD = SHARED + LANES
 BF = jnp.bfloat16
 F32 = jnp.float32
-VMEM_LIMIT = 60 * 2**20
+LIMITS = {"k_final": 60, "k_tokens": 60, "k_sums": 60}
 
 
 def dot_nn(a, b):
@@ -86,8 +86,9 @@
 
 def pack_in_kernel(shared_ref, step_ref, main_ref, out_ref):
     out_ref[:, 0:SHARED] = shared_ref[...]
-    out_ref[:, SHARED:LEAD] = jnp.zeros((out_ref.shape[0], LANES), BF)
-    out_ref[:, SHARED : SHARED + step_ref.shape[1]] = step_ref[...]
+    heads, rows = step_ref.shape
+    tall = jnp.concatenate([step_ref[...].astype(F32), jnp.zeros((LANES - heads, rows), F32)], axis=0)
+    out_ref[:, SHARED:LEAD] = jnp.transpose(tall).astype(BF)
     out_ref[:, LEAD:] = main_ref[0]
 
 
@@ -334,9 +335,19 @@
         hist_ref[pl.ds(k + 1, 1)] = hold[...].astype(BF)[None]
 
 
+def store_halves(outs, *refs):
+    first = pl.program_id(0) < pl.num_programs(0) // 2
+    for here, keep_ref, send_ref in ((first, *refs[:2]), (~first, *refs[2:])):
+
+        @pl.when(here)
+        def _():
+            for q, out in enumerate(outs):
+                (send_ref if q % 2 else keep_ref)[q // 2] = out
+
+
 def gate_kernel(
     idx_ref, own_ref, near_ref, nearx_ref, far_ref, farx_ref, normed_ref, y_ref, cot_ref, gain_ref,
-    gate_ref, gg_ref, out0_ref, out1_ref, out2_ref, out3_ref, stat_ref,
+    gate_ref, gg_ref, keepa_ref, senda_ref, keepb_ref, sendb_ref, stat_ref,
     held, sems,
 ):
     k = pl.program_id(0)
@@ -360,10 +371,11 @@
         gg_ref[:, lanes] = (gated * gain_ref[0:1, lanes]).astype(BF)
         square = square + padded(gated * gated)
     cross = jnp.zeros((STRETCH, LANES), F32)
-    for q, out_ref in enumerate((out0_ref, out1_ref, out2_ref, out3_ref)):
-        a = lax.rem(idx_ref[6] + q, count)
+    outs = []
+    for q in range(count):
+        a = jnp.bitwise_xor(idx_ref[6], q)
         out = dot_nt(gg_ref[...], held[a, :, at_out : at_out + channels])
-        out_ref[...] = out.astype(BF)
+        outs.append(out.astype(BF))
         inner = out * cot_ref[:, pl.ds(pl.multiple_of(a * chunk, LANES), chunk)].astype(F32)
         for part in range(0, chunk, LANES):
             cross = cross + inner[:, part : part + LANES]
@@ -371,6 +383,7 @@
     square = exact(dot_nt, ones, square, 3, False)
     cross = exact(dot_nt, ones, cross, 3, False)
     stat_ref[...] = jnp.where(iota((8, STRETCH), 0) == 0, square, cross)
+    store_halves(outs, keepa_ref, senda_ref, keepb_ref, sendb_ref)
 
 
 def padded(v):
@@ -503,7 +516,7 @@
     gram_bottom = jnp.zeros((HALF, HALF), F32)
     grad_keys = jnp.zeros((STRETCH, STATE), F32)
     grad_queries = jnp.zeros((STRETCH, STATE), F32)
-    rowterm = jnp.zeros((STRETCH, LANES), F32)
+    cumterm = jnp.zeros((STRETCH, LANES), F32)
     colterm = jnp.zeros((STRETCH, LANES), F32)
     endterm = jnp.zeros((8, LANES), F32)
     for pair, (at, width) in enumerate(pair_widths(channels)):
@@ -527,16 +540,19 @@
         after = hold[:, lanes]
         low = after.astype(BF)
         efs = spread(ef, pair, width)
-        grad_xs = grad_xs + dot_nn(keys, low) * efs
+        from_end = dot_nn(keys, low) * efs
+        grad_xs = grad_xs + from_end
         gyr = (gyf * spread(rise, pair, width)).astype(BF)
         xe = (xs.astype(F32) * efs).astype(BF)
         grad_queries = grad_queries + dot_nt(gyr, ht_ref[0, :, lanes])
         grad_keys = grad_keys + dot_nt(xe, low)
-        ended = jnp.sum(after * hn_ref[0, :, lanes].astype(F32), axis=0, keepdims=True)
+        ended = jnp.sum(after * ht_ref[0, :, lanes].astype(F32), axis=0, keepdims=True)
+        ended = ended * fac_ref[0, 0:1, lanes] + jnp.sum(xs.astype(F32) * from_end, axis=0, keepdims=True)
         endterm = endterm + exact(dot_nn, jnp.broadcast_to(ended, (8, width)), expand, 3, True)
         hold[:, lanes] = dot_nn(queries_t, gyr) + fac_ref[0, 0:1, lanes] * after
-        rowterm = rowterm + exact(dot_nn, gyf * (y_ref[:, lanes] - skip * xf), expand, 2, True)
-        colterm = colterm + exact(dot_nn, xf * grad_xs, expand, 2, True)
+        xsf = xs.astype(F32)
+        colterm = colterm + exact(dot_nn, xf * grad_xs, expand, 1, True)
+        cumterm = cumterm + exact(dot_nn, gyf * (y_ref[:, lanes] - skip * xf) - xsf * grad_xs, expand, 2, True)
         skipgrad_ref[0:1, lanes] += jnp.sum(gyf * xf, axis=0, keepdims=True)
         grad_x = grad_xs * spread(step, pair, width) + skip * gyf
         post = grad_x * slope_ref[:, lanes].astype(F32)
@@ -556,7 +572,7 @@
     put(shared, conv_back(post, ext(shared), ks_ref[...], masks, ksgrad_ref, shared))
 
     rate = -jnp.exp(hp_ref[0:1, :])
-    grad_cum = rowterm - step * colterm
+    grad_cum = cumterm
     at_end = iota((STRETCH, LANES), 0) == STRETCH - 1
     grad_cum = grad_cum + jnp.where(at_end, endterm[0:1], 0.0)
     upper = (iota((STRETCH, STRETCH), 1) >= iota((STRETCH, STRETCH), 0)).astype(F32).astype(BF)
@@ -573,11 +589,12 @@
         ghalo_ref[:, SHARED:LEAD] = jnp.zeros((HALO, LANES), BF)
         wide = jnp.broadcast_to(skipgrad_ref[0:1, :], (8, channels))
         small_ref[...] = jnp.zeros_like(small_ref)
-        small_ref[1:6, 0:channels] = kmgrad_ref[0:5, :]
-        small_ref[6:11, 0:SHARED] = ksgrad_ref[0:5, :]
-        small_ref[11:12, 0:channels] = gategrad_ref[0:1, :]
-        small_ref[12:14, 0:LANES] = head_ref[0:2, :]
-        small_ref[14:15, 0:LANES] = exact(dot_nn, wide, expand_ref[...], 3, True)[0:1]
+        for tap in range(5):
+            small_ref[1:2, tap * SHARED : (tap + 1) * SHARED] = ksgrad_ref[tap : tap + 1, :]
+        small_ref[3:8, 0:channels] = kmgrad_ref[0:5, :]
+        small_ref[8:9, 0:channels] = gategrad_ref[0:1, :]
+        small_ref[9:11, 0:LANES] = head_ref[0:2, :]
+        small_ref[11:12, 0:LANES] = exact(dot_nn, wide, expand_ref[...], 3, True)[0:1]
         for copy in copies:
             copy.wait()
         chunk = held.shape[1]
@@ -588,8 +605,8 @@
 def normed_kernel(
     idx_ref, own0_ref, near0_ref, nearx0_ref, far0_ref, farx0_ref, own_ref, near_ref, nearx_ref, far_ref, farx_ref,
     gi_ref, g_ref, normed_ref, back_ref, small_ref,
-    out0_ref, out1_ref, out2_ref, out3_ref, cross_ref, sums_ref,
-    held0, held, sems0, sems, acc,
+    keepa_ref, senda_ref, keepb_ref, sendb_ref, sums_ref, cross_ref,
+    held0, held, sems0, sems,
 ):
     i = pl.program_id(0)
     last = i == pl.num_programs(0) - 1
@@ -604,25 +621,25 @@
         copies += fetches(idx_ref, (own_ref, near_ref, nearx_ref, far_ref, farx_ref), held, sems)
         fetch_all(copies)
         sums_ref[...] = small_ref[...]
+        cross_ref[...] = jnp.zeros_like(cross_ref)
 
     cross = jnp.zeros((rows, LANES), F32)
-    for q, out_ref in enumerate((out0_ref, out1_ref, out2_ref, out3_ref)):
-        a = lax.rem(idx_ref[6] + q, count)
+    outs = []
+    for q in range(count):
+        a = jnp.bitwise_xor(idx_ref[6], q)
         lanes = pl.ds(pl.multiple_of(a * chunk, LANES), chunk)
         width = gi_ref.shape[1]
-        acc[...] = dot_nt(gi_ref[...], held0[a, :, 0:width]) + dot_nt(g_ref[...], held[a])
-
-        @pl.when(last)
-        def _():
-            acc[rows - HALO :, :] += back_ref[:, lanes]
-
-        total = acc[...]
-        out_ref[...] = total.astype(BF)
+        total = dot_nt(gi_ref[...], held0[a, :, 0:width]) + dot_nt(g_ref[...], held[a])
+        tail = total[rows - HALO :] + jnp.where(last, back_ref[:, lanes], 0.0)
+        total = jnp.concatenate([total[: rows - HALO], tail], axis=0)
+        outs.append(total.astype(BF))
         inner = total * normed_ref[:, lanes].astype(F32)
         sums_ref[0:1, lanes] += jnp.sum(inner, axis=0, keepdims=True)
         for part in range(0, chunk, LANES):
             cross = cross + inner[:, part : part + LANES]
-    cross_ref[...] = exact(dot_nt, jnp.ones((8, LANES), BF), cross, 3, False)
+    row = exact(dot_nt, jnp.ones((8, LANES), BF), cross, 3, False)[0:1]
+    cross_ref[2:3, pl.ds(pl.multiple_of(i * rows, LANES), rows)] = row
+    store_halves(outs, keepa_ref, senda_ref, keepb_ref, sendb_ref)
 
 
 def put_chunk(idx_ref, keep_ref, send_ref, lanes, value):
@@ -666,31 +683,80 @@
     put_chunk(idx_ref, keep_ref, send_ref, slice(wide, wide + channels), value)
 
 
-def output_kernel(own_ref, inv_ref, part_ref, right_ref, left_ref, out_ref):
+def final_kernel(idx_ref, *refs):
+    go, w, (main_ref, step_ref, shared_ref, out_ref) = refs[:4], refs[4:8], refs[8:]
+    channels = main_ref.shape[2]
+    wide = go[0].shape[2] // 2
+
+    def total(terms, lanes):
+        value = terms[0][0, :, lanes].astype(F32)
+        for term in terms[1:]:
+            value = value + term[0, :, lanes].astype(F32)
+        return value
+
+    shared_ref[...] = total(w, slice(0, SHARED)).astype(shared_ref.dtype)
+    steps = total(w, slice(SHARED, LEAD))
+    rows = step_ref.shape[1]
+    steps = jnp.concatenate([steps, jnp.zeros((-rows % LANES, LANES), F32)], axis=0)
+    step_ref[...] = jnp.transpose(steps)[0 : step_ref.shape[0], 0:rows]
+    for at, width in pair_widths(channels):
+        lanes = slice(at, at + width)
+        main_ref[0, :, lanes] = total(go, lanes)
+        main_ref[1, :, lanes] = total(w, slice(LEAD + at, LEAD + at + width))
+        out_ref[:, lanes] = total(go, slice(wide + at, wide + at + width))
+
+
+def sums_kernel(sums_ref, gain_ref, *refs):
+    terms, (all_ref, km_ref, ks_ref, head_ref, gate_ref) = refs[:-5], refs[-5:]
+    channels = km_ref.shape[1]
+    over = terms[0][0:2]
+    if len(terms) == 4:
+        over = (over + terms[1][0:2]) + (terms[2][0:2] + terms[3][0:2])
+    all_ref[...] = over[0:1] / gain_ref[...]
+    for tap in range(5):
+        ks_ref[tap : tap + 1, :] = over[1:2, tap * SHARED : (tap + 1) * SHARED]
+    km_ref[...] = sums_ref[3:8, 0:channels]
+    gate_ref[...] = sums_ref[8:9, 0:channels]
+    head_ref[...] = sums_ref[9:12, 0 : head_ref.shape[1]]
+
+
+def output_kernel(own_ref, inv_ref, *refs):
+    out_ref = refs[-1]
     inv = inv_ref[...]
-    for at in range(0, out_ref.shape[1], LANES):
-        lanes = slice(at, at + LANES)
-        total = part_ref[:, lanes].astype(F32) + right_ref[:, lanes].astype(F32)
-        total = (total + left_ref[:, lanes].astype(F32)) * inv
-        out_ref[:, lanes] = (own_ref[:, lanes].astype(F32) + total).astype(BF)
+    for part, (keep_ref, got_ref, far_ref) in enumerate((refs[0:3], refs[3:6])):
+
+        @pl.when(pl.program_id(0) == part)
+        def _():
+            for at in range(0, out_ref.shape[1], LANES):
+                lanes = slice(at, at + LANES)
+                total = keep_ref[0, :, lanes].astype(F32) + got_ref[0, :, lanes].astype(F32)
+                total = (total + far_ref[0, :, lanes].astype(F32)) * inv
+                out_ref[:, lanes] = (own_ref[:, lanes].astype(F32) + total).astype(BF)
 
 
 def tokens_kernel(
-    width, own_ref, cot_ref, inv_ref, cross_ref, gain_ref, part_ref, right_ref, left_ref, out_ref
+    width, own_ref, cot_ref, inv_ref, t0_ref, t1_ref, t2_ref, t3_ref, gain_ref,
+    keepa_ref, gota_ref, fara_ref, keepb_ref, gotb_ref, farb_ref, out_ref,
 ):
     inv = inv_ref[...]
-    pick = (iota((8, LANES), 0) == 0).astype(F32).astype(BF)
-    cross = exact(dot_tn, cross_ref[...], pick, 3, True)
+    pick = (iota((8, LANES), 0) == 2).astype(F32).astype(BF)
+    cross = (t0_ref[...] + t1_ref[...]) + (t2_ref[...] + t3_ref[...])
+    cross = exact(dot_tn, cross, pick, 3, True)
     back = inv * inv * (cross / width)
-    for at in range(0, out_ref.shape[1], LANES):
-        lanes = slice(at, at + LANES)
-        total = part_ref[:, lanes].astype(F32) + right_ref[:, lanes].astype(F32)
-        total = total + left_ref[:, lanes].astype(F32)
-        out_ref[:, lanes] = (
-            inv * gain_ref[0:1, lanes] * total
-            - own_ref[:, lanes].astype(F32) * back
-            + cot_ref[:, lanes].astype(F32)
-        )
+    halves = ((keepa_ref, gota_ref, fara_ref), (keepb_ref, gotb_ref, farb_ref))
+    for part, (keep_ref, got_ref, far_ref) in enumerate(halves):
+
+        @pl.when(pl.program_id(0) == part)
+        def _():
+            for at in range(0, out_ref.shape[1], LANES):
+                lanes = slice(at, at + LANES)
+                total = keep_ref[0, :, lanes].astype(F32) + got_ref[0, :, lanes].astype(F32)
+                total = total + far_ref[0, :, lanes].astype(F32)
+                out_ref[:, lanes] = (
+                    inv * gain_ref[0:1, lanes] * total
+                    - own_ref[:, lanes].astype(F32) * back
+                    + cot_ref[:, lanes].astype(F32)
+                )
 
 
 def whole(array):
@@ -698,7 +764,7 @@
     return pl.BlockSpec(array.shape, lambda *_: (0,) * rank)
 
 
-def call(kernel, grid, ins, in_specs, outs, out_specs, scratch=(), flops=0, prefetch=0):
+def call(name, kernel, grid, ins, in_specs, outs, out_specs, scratch=(), flops=0, prefetch=0):
     moved = sum(a.size * a.dtype.itemsize for a in (*ins, *outs))
     return pl.pallas_call(
         kernel,
@@ -711,7 +777,7 @@
             scratch_shapes=list(scratch),
         ),
         compiler_params=pltpu.CompilerParams(
-            dimension_semantics=("arbitrary",) * len(grid), vmem_limit_bytes=VMEM_LIMIT
+            dimension_semantics=("arbitrary",) * len(grid), vmem_limit_bytes=LIMITS.get(name, 16) * 2**20
         ),
         cost_estimate=pl.CostEstimate(
             flops=int(flops), bytes_accessed=int(moved), transcendentals=0
@@ -761,6 +827,11 @@
         )
         return (v + first) + (second + third)
 
+    def tp_terms(v):
+        if not line:
+            return (lax.psum(v, "tp"),)
+        return (v, *(lax.ppermute(v, "tp", [(i, i ^ m) for i in range(nt)]) for m in (1, 2, 3)))
+
     def one(v, at):
         return lax.dynamic_slice_in_dim(v, at, 1, 0)
 
@@ -784,23 +855,15 @@
         which = iota((2, 1, 1), 0) == c
         near = add(keep[0:2], got[0:2], jnp.where(which, far.astype(F32), 0.0))
         near = lax.ppermute(near, both, role)
-        other = lax.ppermute(one(near, 1 - c), "ctx", swap)
-        own = keep[3].astype(F32) + got[3].astype(F32)
-        return own + one(near, c)[0].astype(F32) + other[0].astype(F32)
-
-    def scatter_tp(pieces):
+        return keep, got, near, lax.ppermute(one(near, 1 - c), "ctx", swap)
+
+    def scatter_tp(keep, send):
         if not line:
-            full = jnp.concatenate(pieces, axis=1)
-            total = lax.psum_scatter(full, "tp", scatter_dimension=1, tiled=True)
-            return total, jnp.zeros_like(total), jnp.zeros_like(total)
-        right = left = None
-        for r in range(1, nt):
-            a, b = pieces[nt - r], pieces[r]
-            if right is not None:
-                a, b = add(a, right), add(b, left)
-            right = lax.ppermute(a, "tp", [(i, i + 1) for i in range(r)])
-            left = lax.ppermute(b, "tp", [(i, i - 1) for i in range(nt - r, nt)])
-        return pieces[0], right, left
+            full = jnp.concatenate([keep[0], send[0], keep[1], send[1]], axis=1)
+            return (lax.psum_scatter(full, "tp", scatter_dimension=1, tiled=True),)
+        got = lax.ppermute(send, "tp", [(i, i ^ 1) for i in range(nt)])
+        far = lax.ppermute(add(keep[1:2], got[1:2]), "tp", [(i, i ^ 2) for i in range(nt)])
+        return keep, got, far
 
     any_spec = pl.BlockSpec(memory_space=pl.ANY)
     sems = pltpu.SemaphoreType.DMA((5,))
@@ -820,14 +883,19 @@
             return pl.BlockSpec((1, rows, columns), lambda i, *_: (nb - 1 - i + off, 0, 0))
         return pl.BlockSpec((1, rows, columns), lambda i, *_: (i + off, 0, 0))
 
+    mid = length // 2
+    part_a = pl.BlockSpec((2, STRETCH, chunk), lambda i, *_: (0, jnp.minimum(i, nb // 2 - 1), 0))
+    part_b = pl.BlockSpec((2, STRETCH, chunk), lambda i, *_: (0, jnp.maximum(i - nb // 2, 0), 0))
+
     def main_part(which):
         return pl.BlockSpec((1, chunk, channels), lambda i: (which, 0, 0))
 
     tokens2, cot2 = tokens[0], cotangent[0]
-    ins = (proj_shared, proj_step, proj_main)
+    step_t = jnp.transpose(proj_step)
+    ins = (proj_shared, step_t, proj_main)
     outs = (shape((chunk, lead), BF),)
     shard_in = call(
-        pack_in_kernel, (1,), ins, [whole(proj_shared), whole(proj_step), main_part(1)],
+        "k_packin", pack_in_kernel, (1,), ins, [whole(proj_shared), whole(step_t), main_part(1)],
         outs, [whole(outs[0])],
     )[0]
     w_in = gather_rows(shard_in, False)
@@ -835,7 +903,7 @@
     ins = (proj_main, output_projection)
     outs = (shape((chunk, 2 * wide), BF),)
     shard_go = call(
-        pack_go_kernel, (1,), ins, [main_part(0), whole(output_projection)],
+        "k_packgo", pack_go_kernel, (1,), ins, [main_part(0), whole(output_projection)],
         outs, [whole(outs[0])],
     )[0]
     w_go = gather_rows(shard_go, True)
@@ -849,7 +917,7 @@
         shape((length, chunk), BF), shape((length, LANES), F32), shape((8, length), F32),
     )
     normed, nhalo, own_tokens, own_cot, inv_rms, tab = call(
-        functools.partial(prep_kernel, chunk), (nb,), ins,
+        "k_prep", functools.partial(prep_kernel, chunk), (nb,), ins,
         [block(width), whole(halo), block(width), whole(gain_row), whole(segments)],
         outs, [block(width), whole(outs[1]), block(chunk), block(chunk), block(LANES), across()], prefetch=1,
     )
@@ -868,7 +936,7 @@
     wide_row = pltpu.VMEM((8, LANES), F32)
     held_in = pltpu.VMEM((nf, chunk, lead), BF)
     pre, phalo, x, xs, slope, bc, slopes, step, cum, sgm, states, fac, total = call(
-        first_kernel, (nb,), ins,
+        "k_first", first_kernel, (nb,), ins,
         [any_spec] * 5
         + [block(width), whole(nhalo), whole(conv_main), whole(conv_shared), whole(head_params), across()],
         outs,
@@ -885,7 +953,7 @@
     outs = (shape((length, channels), F32), shape((nb + 1, STATE, channels), BF))
     ins = (bc, x, xs, cum, states, fac, enter, head_params, tab)
     y, hist = call(
-        second_kernel, (nb,), ins,
+        "k_second", second_kernel, (nb,), ins,
         [
             block(SHARED), block(channels), block(channels), block(LANES), stacked(STATE, channels),
             stacked(8, channels), whole(enter), whole(head_params), across(),
@@ -895,20 +963,24 @@
         flops=8 * length * STRETCH * channels,
     )
 
-    outs = (shape((length, channels), BF),) * 2 + (shape((length, chunk), BF),) * nf + (shape((8, length), F32),)
+    outs = (
+        shape((length, channels), BF), shape((length, channels), BF), *(shape((2, mid, chunk), BF),) * 4,
+        shape((8, length), F32),
+    )
     ins = (idx, *w_go, normed, y, cot2, gate_row)
     gate, gg, *out_parts, stat = call(
-        gate_kernel, (nb,), ins,
+        "k_gate", gate_kernel, (nb,), ins,
         [any_spec] * 5 + [block(width), block(channels), block(width), whole(gate_row)],
-        outs, [block(channels)] * 2 + [block(chunk)] * nf + [across()],
+        outs, [block(channels)] * 2 + [part_a, part_a, part_b, part_b, across()],
         scratch=[pltpu.VMEM((nf, chunk, 2 * wide), BF), sems],
         prefetch=1, flops=4 * length * width * channels,
     )
-    out_terms = scatter_tp(out_parts)
+    out_a = scatter_tp(*out_parts[:2])
+    out_b = scatter_tp(*out_parts[2:])
     stat = tp_sum(stat)
     outs = (shape((length, channels), BF),)
     gng = call(
-        gng_kernel, (nb,), (idx, *w_go, cot2), [any_spec] * 5 + [block(width)], outs, [block(channels)],
+        "k_gng", gng_kernel, (nb,), (idx, *w_go, cot2), [any_spec] * 5 + [block(width)], outs, [block(channels)],
         scratch=[pltpu.VMEM((nf, chunk, wide), BF), sems], prefetch=1, flops=2 * length * width * channels,
     )[0]
 
@@ -918,7 +990,7 @@
     )
     ins = (stat, y, gate, gng, gate_row, bc, cum, fac, tab)
     gy, gi, inv_gate, flow, gate_grad = call(
-        third_kernel, (nb,), ins,
+        "k_third", third_kernel, (nb,), ins,
         [
             across(True), block(channels, True), block(channels, True), block(channels, True), whole(gate_row),
             block(SHARED, True), block(LANES, True), stacked(8, channels, True), across(True),
@@ -932,7 +1004,7 @@
     outs = (shape((4, half, 2 * wide), BF),) * 2
     ins = (idx, normed, gi, cot2, inv_gate, gg)
     grad_go = call(
-        gate_out_kernel, (nf,), ins,
+        "k_go", gate_out_kernel, (nf,), ins,
         [
             pl.BlockSpec((length, chunk), lambda i, *_: (0, i)), whole(gi),
             pl.BlockSpec((length, chunk), lambda i, *_: (0, i)), whole(inv_gate), whole(gg),
@@ -951,7 +1023,7 @@
     )
     per_block = STRETCH // HALO
     g_in, ghalo, small, back = call(
-        fourth_kernel, (nb,), ins,
+        "k_fourth", fourth_kernel, (nb,), ins,
         [any_spec] * 5
         + [block(channels, True)] * 5 + [block(SHARED, True)] * 2 + [block(LANES, True)] * 3
         + [
@@ -971,23 +1043,21 @@
     )
     back = lax.ppermute(back, "ctx", [(1, 0)])
 
-    outs = (shape((length, chunk), BF),) * nf + (shape((8, length), F32), shape((16, width), F32))
+    outs = (shape((2, mid, chunk), BF),) * 4 + (shape((16, width), F32), shape((8, width), F32))
     ins = (idx, *w_go, *w_in, gi, g_in, normed, back, small)
-    *normed_parts, cross, sums = call(
-        normed_kernel, (nb,), ins,
+    keep_a, send_a, keep_b, send_b, sums, cross = call(
+        "k_normed", normed_kernel, (nb,), ins,
         [any_spec] * 10 + [block(channels), block(lead), block(width), whole(back), whole(small)],
-        outs, [block(chunk)] * nf + [across(), whole(outs[-1])],
-        scratch=[
-            pltpu.VMEM((nf, chunk, wide), BF), held_in, sems, sems, pltpu.VMEM((STRETCH, chunk), F32),
-        ],
+        outs, [part_a, part_a, part_b, part_b, whole(outs[-2]), whole(outs[-1])],
+        scratch=[pltpu.VMEM((nf, chunk, wide), BF), held_in, sems, sems],
         prefetch=1, flops=2 * length * width * (lead + channels),
     )
-    normed_terms = scatter_tp(normed_parts)
-    cross = tp_sum(cross)
+    normed_a = scatter_tp(keep_a, send_a)
+    normed_b = scatter_tp(keep_b, send_b)
 
     outs = (shape((4, half, lead), BF),) * 2
     grad_w = call(
-        weight_kernel, (nf,), (idx, normed, nhalo, g_in, ghalo),
+        "k_weight", weight_kernel, (nf,), (idx, normed, nhalo, g_in, ghalo),
         [
             pl.BlockSpec((length, chunk), lambda i, *_: (0, i)), pl.BlockSpec((HALO, chunk), lambda i, *_: (0, i)),
             whole(g_in), whole(ghalo),
@@ -1000,49 +1070,71 @@
     sums = sums + lax.ppermute(sums, "ctx", swap)
     for m in (1, 2):
         sums = sums + lax.ppermute(sums, "fsdp", [(i, i ^ m) for i in range(nf)])
-    over_tp = tp_sum(sums)
+    sum_terms = tp_terms(jnp.where(iota((8, 1), 0) < 2, sums[:8], cross))
+    outs = (
+        shape((1, width), F32), shape((5, channels), F32), shape((5, SHARED), F32), shape((3, heads), F32),
+        shape((1, channels), F32),
+    )
+    ins = (sums, gain_row, *sum_terms)
+    gain_all, grad_km, grad_ks, grad_head, grad_gate = call(
+        "k_sums", sums_kernel, (1,), ins, [whole(v) for v in ins], outs, [whole(o) for o in outs]
+    )
+    grad_gain = lax.dynamic_slice_in_dim(gain_all[0], t * share, share, 0)
     own_gain = lax.dynamic_slice_in_dim(norm_gain, t * share, share, 0)
-    grad_gain = lax.dynamic_slice_in_dim(over_tp[0], t * share, share, 0) / own_gain
+
+    def terms_of(columns):
+        return [
+            pl.BlockSpec((1, half, columns), lambda i, *_: (3, 0, 0)),
+            pl.BlockSpec((1, half, columns), lambda i, *_: (3, 0, 0)),
+            pl.BlockSpec((1, half, columns), lambda i, idx_ref: (idx_ref[4], 0, 0)),
+            pl.BlockSpec((1, half, columns), lambda i, *_: (0, 0, 0)),
+        ]
+
+    outs = (
+        shape((2, half, channels), F32), shape((heads, half), F32), shape((half, SHARED), BF if line else F32),
+        shape((half, channels), F32),
+    )
+    grad_main, grad_step, grad_shared, grad_out = call(
+        "k_final", final_kernel, (1,), (idx, *grad_go, *grad_w), terms_of(2 * wide) + terms_of(lead),
+        outs, [whole(o) for o in outs], prefetch=1,
+    )
+    grad_shared = [v.astype(F32) for v in tp_terms(grad_shared)]
+    if line:
+        grad_shared = [(grad_shared[0] + grad_shared[1]) + (grad_shared[2] + grad_shared[3])]
 
     outs = (shape((length, share), BF),)
     if line:
-        spec = pl.BlockSpec((length // 2, share), lambda i: (i, 0))
-        inv_spec = pl.BlockSpec((length // 2, LANES), lambda i: (i, 0))
+        spec = pl.BlockSpec((mid, share), lambda i: (i, 0))
+        only = pl.BlockSpec((1, mid, share), lambda i: (0, 0, 0))
+        inv_spec = pl.BlockSpec((mid, LANES), lambda i: (i, 0))
         output = call(
-            output_kernel, (2,), (own_tokens, inv_gate, *out_terms), [spec, inv_spec, spec, spec, spec],
+            "k_output", output_kernel, (2,), (own_tokens, inv_gate, *out_a, *out_b), [spec, inv_spec] + [only] * 6,
             outs, [spec],
         )[0]
         outs = (shape((length, share), F32),)
         gain2 = own_gain[None]
         grad_tokens = call(
-            functools.partial(tokens_kernel, width), (2,),
-            (own_tokens, own_cot, inv_rms, cross, gain2, *normed_terms),
-            [
-                spec, spec, inv_spec, pl.BlockSpec((8, length // 2), lambda i: (0, i)), whole(gain2), spec, spec,
-                spec,
-            ],
+            "k_tokens", functools.partial(tokens_kernel, width), (2,),
+            (own_tokens, own_cot, inv_rms, *sum_terms, gain2, *normed_a, *normed_b),
+            [spec, spec, inv_spec]
+            + [pl.BlockSpec((8, mid), lambda i: (0, i))] * 4
+            + [whole(gain2)]
+            + [only] * 6,
             outs, [spec],
         )[0]
     else:
-        output = (own_tokens.astype(F32) + inv_gate[:, :1] * out_terms[0].astype(F32)).astype(BF)
+        normed_sum = jnp.concatenate([normed_a[0], normed_b[0]], axis=0).astype(F32)
+        out_sum = jnp.concatenate([out_a[0], out_b[0]], axis=0).astype(F32)
+        output = (own_tokens.astype(F32) + inv_gate[:, :1] * out_sum).astype(BF)
         inv = inv_rms[:, :1]
         grad_tokens = (
-            inv * own_gain * normed_terms[0].astype(F32)
-            - own_tokens.astype(F32) * (inv * inv * (cross[0][:, None] / width))
+            inv * own_gain * normed_sum
+            - own_tokens.astype(F32) * (inv * inv * (sum_terms[0][2, :length, None] / width))
             + own_cot.astype(F32)
         )
     return (
-        output[None],
-        grad_tokens[None],
-        grad_gain,
-        jnp.stack([grad_go[:, :channels], grad_w[:, LEAD:]]),
-        tp_sum(grad_w[:, :SHARED]),
-        grad_w[:, SHARED : SHARED + heads],
-        sums[1:6, :channels],
-        over_tp[6:11, :SHARED],
-        sums[12:15, :heads],
-        sums[11, :channels],
-        jnp.transpose(grad_go[:, wide : wide + channels]),
+        output[None], grad_tokens[None], grad_gain, grad_main, grad_shared[0], jnp.transpose(grad_step), grad_km,
+        grad_ks, grad_head, grad_gate[0], jnp.transpose(grad_out),
     )
 
 

time: 364 us -> 348 us (0.956)
  Pallas kernels: 148 us -> 120 us
  waiting for transfers between devices: 85.5 us -> 105 us
  other arithmetic: 21.6 us -> 12.8 us
  local copies, waits for them, and re-layouts: 17.2 us -> 23.3 us
    ppermute x14 -> x16, waiting for transfers between devices: 20.1 us -> 56.4 us  [the longest x6 37.6 us: tp_terms(): lax.ppermute(v, 'tp', [(i, i ^ m) for i in range(nt)])]
    ppermute x12 -> x3, starting transfers between devices: 38.6 us -> 5.1 us  [tp_sum(): lax.ppermute(v, 'tp', [(i, i ^ m) for i in range(nt)])]
    ppermute x14 -> x16, starting transfers between devices: 25.8 us -> 55 us  [the longest x6 44.7 us: tp_terms(): lax.ppermute(v, 'tp', [(i, i ^ m) for i in range(nt)])]
    pallas_call x14 -> x16, Pallas kernels: 148 us -> 120 us  [call(): pl.pallas_call(kernel, out_shape=outs, grid_spec=pltpu.PrefetchScalarGrid...]
    ppermute x12 -> x3, waiting for transfers between devices: 18.8 us -> 0.01 us  [tp_sum(): lax.ppermute(v, 'tp', [(i, i ^ m) for i in range(nt)])]
    unnamed x50 -> x112, local copies, waits for them, and re-layouts: 6.77 us -> 16.7 us
    ppermute x2, waiting for transfers between devices: 0.35 us -> 4.02 us  [per_device(): sums = sums + lax.ppermute(sums, 'fsdp', [(i, i ^ m) for i in range(nf)])]
    convert_element_type x10 -> x8, other arithmetic: 13.1 us -> 9.49 us  [add(): return sum((term.astype(F32) for term in terms)).astype(BF)]
  transfers between devices with their start and end apart: 47 -> 40, of which waited for: 17 -> 15; matrix products, arithmetic and copies ran while one was open for 8% -> 5% of each run, Pallas kernels for 22% -> 29%
where the time goes in v1:
time: 348 us; the launch traced here: 347 us
  Pallas kernels  120 us (34%)
  waiting for transfers between devices  105 us (30%)
  starting transfers between devices  85.2 us (24%)
  local copies, waits for them, and re-layouts  23.3 us (7%)
  other arithmetic  12.8 us (4%)
    pallas_call x16, Pallas kernels, call(): pl.pallas_call(kernel, out_shape=outs, grid_spec=pltpu.PrefetchScalarGrid...  120 us
    ppermute x6, starting transfers between devices, tp_terms(): lax.ppermute(v, 'tp', [(i, i ^ m) for i in range(nt)])  44.7 us
    ppermute x6, waiting for transfers between devices, tp_terms(): lax.ppermute(v, 'tp', [(i, i ^ m) for i in range(nt)])  37.6 us
    ppermute x2, waiting for transfers between devices, gather_rows(): near = lax.ppermute(pieces, both, role)  25 us
    ppermute x4, waiting for transfers between devices, scatter_tp(): got = lax.ppermute(send, 'tp', [(i, i ^ 1) for i in range(nt)])  18.8 us
    unnamed x112, local copies, waits for them, and re-layouts  16.7 us
    ppermute x2, waiting for transfers between devices, scatter_rows(): far = lax.ppermute(add(keep[2:3], got[2:3]), both, turn)  13.2 us
    convert_element_type x8, other arithmetic, add(): return sum((term.astype(F32) for term in terms)).astype(BF)  9.49 us
  transfers between devices with their start and end apart: 40, of which 15 were waited for; matrix products, arithmetic and copies ran while one was open for 5% of the time, Pallas kernels for 29%

profile of v1, /device:TPU:0, one launch (start us, length us, event | category | flops | bytes accessed | tf_op | source)
XLA Modules:
  0.0 347.0 jit_solution(9726289253826118632)
XLA Ops:
  4.6 3.0 collective-permute-start.5
  9.5 9.4 %collective-permute-done.5 = bf16[2,192,1152]{2,1,0:T(8,128)(2,1)} collective-permute-done((bf16[2,192,1152]{2,1,0:T(8,128)(2,1)}, bf16[2,192,1152]{2,1,0:T(8,128)(2,1)}, u32[]{:S(2)}, u32[]{:S(2)}) %collective-permute-start.5) | collective-permute-done | bytes 884768 | tf_op jit(solution)/shard_map/ppermute | solution.py:841
  25.4 15.7 %collective-permute-done.1 = bf16[2,192,1536]{2,1,0:T(8,128)(2,1)} collective-permute-done((bf16[2,192,1536]{2,1,0:T(8,128)(2,1)}, bf16[2,192,1536]{2,1,0:T(8,128)(2,1)}, u32[]{:S(2)}, u32[]{:S(2)}) %collective-permute-start.1) | collective-permute-done | bytes 1179680 | tf_op jit(solution)/shard_map/ppermute | solution.py:841
  52.4 16.9 %shard_map.206 = (bf16[1024,1152]{1,0:T(8,128)(2,1)S(1)}, bf16[16,1152]{1,0:T(8,128)(2,1)S(1)}, bf16[1024,768]{1,0:T(8,128)(2,1)S(1)}, bf16[1024,768]{1,0:T(8,12...) custom-call(s32[8]{0:T(128)S(1)} %stack.29.idx_ref, ...), custom_call_target="tpu_custom_call" | custom-call | flops 3825205248 | bytes 18391216 | tf_op jit(solution)/shard_map/pallas_call | solution.py:769
  72.4 6.1 %shard_map.207 = (f32[1024,768]{1,0:T(8,128)S(1)}, bf16[5,128,768]{2,1,0:T(8,128)(2,1)S(1)}) custom-call(bf16[1024,256]{1,0:T(8,128)(2,1)S(1)} %get-tuple-element.71.bc_ref, bf16[1024,768]{1,0:T(8,128)(2,1)S(1)} %get-tuple-element.72.x_ref, bf16[1024,768]{1,0:T(8,128)(2,1)S(1)} %get-tuple-element.73.xs_ref, f32[1024,128]{1,0:T(8,128)S(1)} %get-tuple-element.74.cum_ref, ...), custom_call_target="tpu_custom_call" | custom-call | flops 1610612736 | bytes 10223760 | tf_op jit(solution)/shard_map/pallas_call | solution.py:769
  78.6 13.7 %shard_map.208 = (bf16[1024,768]{1,0:T(8,128)(2,1)S(1)}, bf16[1024,768]{1,0:T(8,128)(2,1)S(1)}, bf16[2,512,384]{2,1,0:T(8,128)(2,1)S(1)}, bf16[2,512,384]{2,1,0:...) custom-call(s32[8]{0:T(128)S(1)} %stack.29.idx_ref, ...), custom_call_target="tpu_custom_call" | custom-call | flops 4831838208 | bytes 20483104 | tf_op jit(solution)/shard_map/pallas_call | solution.py:769
  97.4 6.0 %shard_map.209.gng_ref = bf16[1024,768]{1,0:T(8,128)(2,1)S(1)} custom-call(s32[8]{0:T(128)S(1)} %stack.29.idx_ref, bf16[384,1536]{1,0:T(8,128)(2,1)} %shard_map.204.own_ref.own0_ref, bf16[384,1536]{1,0:T(8,128)(2,1)} %bitcast.10.near_ref.near0_ref, bf16[384,1536]{1,0:T(8,128)(2,1)} %bitcast.11.nearx_ref.nearx0_ref, ...), custom_call_target="tpu_custom_call" | custom-call | flops 2415919104 | bytes 9437216 | tf_op jit(solution)/shard_map/pallas_call | solution.py:769
  103.5 5.2 %shard_map.210 = (bf16[1024,768]{1,0:T(8,128)(2,1)S(1)}, bf16[1024,768]{1,0:T(8,128)(2,1)S(1)}, f32[1024,128]{1,0:T(8,128)S(1)}, bf16[128,768]{1,0:T(8,128)(2,1)S(1)}, f32[8,768]{1,0:T(8,128)S(1)}) custom-call(f32[8,1024]{1,0:T(8,128)S(1)} %add_add_fusion.1.stat_ref, f32[1024,768]{1,0:T(8,128)S(1)} %get-tuple-element.78.y_ref, ...), custom_call_target="tpu_custom_call" | custom-call | flops 201326592 | bytes 11398144 | tf_op jit(solution)/shard_map/pallas_call | solution.py:769
  110.2 11.6 %shard_map.216 = (bf16[4,192,1536]{2,1,0:T(8,128)(2,1)S(1)}, bf16[4,192,1536]{2,1,0:T(8,128)(2,1)}) custom-call(s32[8]{0:T(128)S(1)} %stack.29.idx_ref, bf16[1024,1536]{1,0:T(8,128)(2,1)S(1)} %get-tuple-element.68.normed_ref, bf16[1024,768]{1,0:T(8,128)(2,1)S(1)} %get-tuple-element.88.gi_ref, bf16[1024,1536]{1,0:T(8,128)(2,1)S(1)} %bitcast.34, ...), custom_call_target="tpu_custom_call" | custom-call | flops 4831838208 | bytes 14680096 | tf_op jit(solution)/shard_map/pallas_call | solution.py:769
  124.3 21.3 %shard_map.212 = (bf16[1024,1152]{1,0:T(8,128)(2,1)S(1)}, bf16[16,1152]{1,0:T(8,128)(2,1)S(1)}, f32[16,1536]{1,0:T(8,128)S(1)}, f32[16,1536]{1,0:T(8,128)S(1)}) custom-call(s32[8]{0:T(128)S(1)} %stack.29.idx_ref, bf16[384,1152]{1,0:T(8,128)(2,1)} %shard_map.205.own_ref, bf16[384,1152]{1,0:T(8,128)(2,1)} %bitcast.16.near_ref, ...), custom_call_target="tpu_custom_call" | custom-call | flops 3221225472 | bytes 25284784 | tf_op jit(solution)/shard_map/pallas_call | solution.py:769
  145.6 8.6 %shard_map.217 = (bf16[4,192,1152]{2,1,0:T(8,128)(2,1)S(1)}, bf16[4,192,1152]{2,1,0:T(8,128)(2,1)}) custom-call(s32[8]{0:T(128)S(1)} %stack.29.idx_ref, bf16[1024,1536]{1,0:T(8,128)(2,1)S(1)} %get-tuple-element.68.normed_ref, bf16[16,1536]{1,0:T(8,128)(2,1)S(1)} %get-tuple-element.69.nhalo_ref, bf16[1024,1152]{1,0:T(8,128)(2,1)S(1)} %get-tuple-element.99.g_ref, ...), custom_call_target="tpu_custom_call" | custom-call | flops 3623878656 | bytes 9130016 | tf_op jit(solution)/shard_map/pallas_call | solution.py:769
  159.5 14.1 %shard_map.213 = (bf16[2,512,384]{2,1,0:T(8,128)(2,1)S(1)}, bf16[2,512,384]{2,1,0:T(8,128)(2,1)S(1)}, bf16[2,512,384]{2,1,0:T(8,128)(2,1)S(1)}, bf16[2,512,384]{...) custom-call(s32[8]{0:T(128)S(1)} %stack.29.idx_ref, ...), custom_call_target="tpu_custom_call" | custom-call | flops 6039797760 | bytes 18825248 | tf_op jit(solution)/shard_map/pallas_call | solution.py:769
  179.3 3.2 collective-permute-done.20
  192.8 5.0 %collective-permute-done.34 = bf16[1,192,1152]{2,1,0:T(8,128)(2,1)S(1)} collective-permute-done((bf16[1,192,1152]{2,1,0:T(8,128)(2,1)S(1)}, bf16[1,192,1152]{2,1,0:T(8,128)(2,1)S(1)}, u32[]{:S(2)}, u32[]{:S(2)}) %collective-permute-start.34) | collective-permute-done | bytes 442400 | tf_op jit(solution)/shard_map/ppermute | solution.py:854
  201.0 8.2 %collective-permute-done.30 = bf16[1,192,1536]{2,1,0:T(8,128)(2,1)S(1)} collective-permute-done((bf16[1,192,1536]{2,1,0:T(8,128)(2,1)S(1)}, bf16[1,192,1536]{2,1,0:T(8,128)(2,1)S(1)}, u32[]{:S(2)}, u32[]{:S(2)}) %collective-permute-start.30) | collective-permute-done | bytes 589856 | tf_op jit(solution)/shard_map/ppermute | solution.py:854
  215.2 6.6 %collective-permute-done.13.refs_1_ = bf16[2,512,384]{2,1,0:T(8,128)(2,1)S(1)} collective-permute-done((bf16[2,512,384]{2,1,0:T(8,128)(2,1)}, bf16[2,512,384]{2,1,0:T(8,128)(2,1)S(1)}, u32[]{:S(2)}, u32[]{:S(2)}) %collective-permute-start.13) | collective-permute-done | bytes 786464 | tf_op jit(solution)/shard_map/ppermute | solution.py:864
  223.3 3.5 %collective-permute-start.23 = (f32[8,1536]{1,0:T(8,128)S(1)}, f32[8,1536]{1,0:T(8,128)S(1)}, u32[]{:S(2)}, u32[]{:S(2)}) collective-permute-start(f32[8,1536]{1,0:T(8,128)S(1)} %slice_select_fusion.t0_ref.refs_0_), channel_id=1, source_target_pairs={{0,2},{1,3},{2,0},{3,1},{4,6},{5,7},{6,4},{7,5},{8,10},{9,11},{10,... | collective-permute-start | bytes 147464 | tf_op jit(solution)/shard_map/ppermute | solution.py:833
  227.6 12.1 %collective-permute-done.27.gotb_ref = bf16[2,512,384]{2,1,0:T(8,128)(2,1)S(1)} collective-permute-done((bf16[2,512,384]{2,1,0:T(8,128)(2,1)}, bf16[2,512,384]{2,1,0:T(8,128)(2,1)S(1)}, u32[]{:S(2)}, u32[]{:S(2)}) %collective-permute-start.27) | collective-permute-done | bytes 786464 | tf_op jit(solution)/shard_map/ppermute | solution.py:864
  240.7 14.9 %collective-permute-done.22.t1_ref.refs_1_ = f32[8,1536]{1,0:T(8,128)S(1)} collective-permute-done((f32[8,1536]{1,0:T(8,128)S(1)}, f32[8,1536]{1,0:T(8,128)S(1)}, u32[]{:S(2)}, u32[]{:S(2)}) %collective-permute-start.22) | collective-permute-done | bytes 49184 | tf_op jit(solution)/shard_map/ppermute | solution.py:833
  262.6 3.7 %collective-permute-start.24 = (f32[8,1536]{1,0:T(8,128)S(1)}, f32[8,1536]{1,0:T(8,128)S(1)}, u32[]{:S(2)}, u32[]{:S(2)}) collective-permute-start(f32[8,1536]{1,0:T(8,128)S(1)} %slice_select_fusion.t0_ref.refs_0_), channel_id=1, source_target_pairs={{0,3},{1,2},{2,1},{3,0},{4,7},{5,6},{6,5},{7,4},{8,11},{9,10},{10,... | collective-permute-start | bytes 147464 | tf_op jit(solution)/shard_map/ppermute | solution.py:833
  266.3 4.5 %shard_map.218 = (f32[2,192,768]{2,1,0:T(8,128)}, f32[12,192]{1,0:T(8,128)}, bf16[192,256]{1,0:T(8,128)(2,1)}, f32[192,768]{1,0:T(8,128)}) custom-call(s32[8]{0:T(128)} %copy-done.33, bf16[4,192,1536]{2,1,0:T(8,128)(2,1)} %copy-done.1, bf16[4,192,1536]{2,1,0:T(8,128)(2,1)} %collective-permute-done.29.refs_1_, bf16[2,192,1536]{2,1,0:T(8,128)(2,1)} %copy-done.43, ...), custom_call_target="tpu_custom_call" | custom-call | bytes 13231136 | tf_op jit(solution)/shard_map/pallas_call | solution.py:769
  270.7 22.6 %collective-permute-done.24.t3_ref.refs_3_ = f32[8,1536]{1,0:T(8,128)S(1)} collective-permute-done((f32[8,1536]{1,0:T(8,128)S(1)}, f32[8,1536]{1,0:T(8,128)S(1)}, u32[]{:S(2)}, u32[]{:S(2)}) %collective-permute-start.24) | collective-permute-done | bytes 49184 | tf_op jit(solution)/shard_map/ppermute | solution.py:833
  293.4 34.3 %collective-permute-start.37 = (bf16[192,256]{1,0:T(8,128)(2,1)}, bf16[192,256]{1,0:T(8,128)(2,1)}, u32[]{:S(2)}, u32[]{:S(2)}) collective-permute-start(bf16[192,256]{1,0:T(8,128)(2,1)} %get-tuple-element.116), channel_id=1, source_target_pairs={{0,1},{1,0},{2,3},{3,2},{4,5},{5,4},{6,7},{7,6},{8,9},{9,8},{10,11... | collective-permute-start | bytes 294920 | tf_op jit(solution)/shard_map/ppermute | solution.py:833
  340.9 4.4 %shard_map.214 = f32[1024,384]{1,0:T(8,128)} custom-call(bf16[1024,384]{1,0:T(8,128)(2,1)} %copy-done.8, bf16[1024,384]{1,0:T(8,128)(2,1)} %copy-done.23, f32[1024,128]{1,0:T(8,128)} %copy-done.25, f32[8,1536]{1,0:T(8,128)} %copy-done.48, f32[8,1536]{1,0:T(8,128)} %copy-done.50, f32[8,1536]{1,0:T(8,128)} %copy-done.51, f32[8,1536]{1,0:T(8,128)} %copy-done.52, ...), custom_call_target="tpu_custom_call" | custom-call | bytes 7800320 | tf_op jit(solution)/shard_map/pallas_call | solution.py:769
  (214 shorter events, 91.3 us)
Async XLA Ops:
  8.8 32.2 %collective-permute-start.1 = (bf16[2,192,1536]{2,1,0:T(8,128)(2,1)}, bf16[2,192,1536]{2,1,0:T(8,128)(2,1)}, u32[]{:S(2)}, u32[]{:S(2)}) collective-permute-start(bf16[2,192,1536]{2,1,0:T(8,128)(2,1)} %bitcast.9), channel_id=1, source_target_pairs={{0,8},{4,20},{8,0},{12,28},{16,24},{20,4},{24,16},{28,12},{1,9},{5... | collective-permute-start | bytes 3538952 | tf_op jit(solution)/shard_map/ppermute | solution.py:841
  19.9 21.1 %collective-permute-start.7 = (bf16[1,192,1152]{2,1,0:T(8,128)(2,1)S(1)}, bf16[1,192,1152]{2,1,0:T(8,128)(2,1)}, u32[]{:S(2)}, u32[]{:S(2)}) collective-permute-start(bf16[1,192,1152]{2,1,0:T(8,128)(2,1)S(1)} %constant_dynamic-slice_fusion.2), channel_id=1, source_target_pairs={{0,16},{4,12},{8,24},{12,4},{16,0},{20,28},{24,8},{28,20},{1,17},{... | collective-permute-start | bytes 1327112 | tf_op jit(solution)/shard_map/ppermute | solution.py:845
  22.0 30.3 %collective-permute-start.6 = (bf16[2,192,1152]{2,1,0:T(8,128)(2,1)}, bf16[2,192,1152]{2,1,0:T(8,128)(2,1)}, u32[]{:S(2)}, u32[]{:S(2)}) collective-permute-start(bf16[2,192,1152]{2,1,0:T(8,128)(2,1)} %collective-permute-done.5), channel_id=1, source_target_pairs={{0,4},{4,0},{1,5},{5,1},{2,6},{6,2},{3,7},{7,3},{8,12},{12,8},{9,1... | collective-permute-start | bytes 2654216 | tf_op jit(solution)/shard_map/ppermute | solution.py:846
  24.0 28.0 %collective-permute-start.3 = (bf16[1,192,1536]{2,1,0:T(8,128)(2,1)}, bf16[1,192,1536]{2,1,0:T(8,128)(2,1)}, u32[]{:S(2)}, u32[]{:S(2)}) collective-permute-start(bf16[1,192,1536]{2,1,0:T(8,128)(2,1)} %constant_dynamic-slice_fusion.3), channel_id=1, source_target_pairs={{0,24},{4,28},{8,16},{12,20},{16,8},{20,12},{24,0},{28,4},{1,25},{... | collective-permute-start | bytes 1769480 | tf_op jit(solution)/shard_map/ppermute | solution.py:843
  41.0 37.5 %collective-permute-start.2 = (bf16[2,192,1536]{2,1,0:T(8,128)(2,1)}, bf16[2,192,1536]{2,1,0:T(8,128)(2,1)}, u32[]{:S(2)}, u32[]{:S(2)}) collective-permute-start(bf16[2,192,1536]{2,1,0:T(8,128)(2,1)} %collective-permute-done.1), channel_id=1, source_target_pairs={{0,4},{4,0},{1,5},{5,1},{2,6},{6,2},{3,7},{7,3},{8,12},{12,8},{9,1... | collective-permute-start | bytes 3538952 | tf_op jit(solution)/shard_map/ppermute | solution.py:846
  52.0 26.5 %collective-permute-start.4 = (bf16[1,192,1536]{2,1,0:T(8,128)(2,1)}, bf16[1,192,1536]{2,1,0:T(8,128)(2,1)S(1)}, u32[]{:S(2)}, u32[]{:S(2)}) collective-permute-start(bf16[1,192,1536]{2,1,0:T(8,128)(2,1)} %collective-permute-done.3), channel_id=1, source_target_pairs={{0,4},{4,0},{1,5},{5,1},{2,6},{6,2},{3,7},{7,3},{8,12},{12,8},{9,1... | collective-permute-start | bytes 1769480 | tf_op jit(solution)/shard_map/ppermute | solution.py:847
  123.2 67.8 %collective-permute-start.29 = (bf16[4,192,1536]{2,1,0:T(8,128)(2,1)}, bf16[4,192,1536]{2,1,0:T(8,128)(2,1)}, u32[]{:S(2)}, u32[]{:S(2)}) collective-permute-start(bf16[4,192,1536]{2,1,0:T(8,128)(2,1)} %get-tuple-element.111), channel_id=1, source_target_pairs={{0,4},{4,0},{1,5},{5,1},{2,6},{6,2},{3,7},{7,3},{8,12},{12,8},{9,1... | collective-permute-start | bytes 7077896 | tf_op jit(solution)/shard_map/ppermute | solution.py:853
  155.5 32.7 %collective-permute-start.33 = (bf16[4,192,1152]{2,1,0:T(8,128)(2,1)}, bf16[4,192,1152]{2,1,0:T(8,128)(2,1)}, u32[]{:S(2)}, u32[]{:S(2)}) collective-permute-start(bf16[4,192,1152]{2,1,0:T(8,128)(2,1)} %get-tuple-element.114), channel_id=1, source_target_pairs={{0,4},{4,0},{1,5},{5,1},{2,6},{6,2},{3,7},{7,3},{8,12},{12,8},{9,1... | collective-permute-start | bytes 5308424 | tf_op jit(solution)/shard_map/ppermute | solution.py:853
  184.3 28.6 %collective-permute-start.15 = (bf16[2,512,384]{2,1,0:T(8,128)(2,1)}, bf16[2,512,384]{2,1,0:T(8,128)(2,1)S(1)}, u32[]{:S(2)}, u32[]{:S(2)}) collective-permute-start(bf16[2,512,384]{2,1,0:T(8,128)(2,1)} %copy-done.39), channel_id=1, source_target_pairs={{0,1},{1,0},{2,3},{3,2},{4,5},{5,4},{6,7},{7,6},{8,9},{9,8},{10,11... | collective-permute-start | bytes 2359304 | tf_op jit(solution)/shard_map/ppermute | solution.py:864
  185.0 36.8 %collective-permute-start.13 = (bf16[2,512,384]{2,1,0:T(8,128)(2,1)}, bf16[2,512,384]{2,1,0:T(8,128)(2,1)S(1)}, u32[]{:S(2)}, u32[]{:S(2)}) collective-permute-start(bf16[2,512,384]{2,1,0:T(8,128)(2,1)} %copy-done.38), channel_id=1, source_target_pairs={{0,1},{1,0},{2,3},{3,2},{4,5},{5,4},{6,7},{7,6},{8,9},{9,8},{10,11... | collective-permute-start | bytes 2359304 | tf_op jit(solution)/shard_map/ppermute | solution.py:864
  187.2 52.5 %collective-permute-start.27 = (bf16[2,512,384]{2,1,0:T(8,128)(2,1)}, bf16[2,512,384]{2,1,0:T(8,128)(2,1)S(1)}, u32[]{:S(2)}, u32[]{:S(2)}) collective-permute-start(bf16[2,512,384]{2,1,0:T(8,128)(2,1)} %copy-done.42), channel_id=1, source_target_pairs={{0,1},{1,0},{2,3},{3,2},{4,5},{5,4},{6,7},{7,6},{8,9},{9,8},{10,11... | collective-permute-start | bytes 2359304 | tf_op jit(solution)/shard_map/ppermute | solution.py:864
  199.4 23.9 %collective-permute-start.35 = (bf16[2,192,1152]{2,1,0:T(8,128)(2,1)S(1)}, bf16[2,192,1152]{2,1,0:T(8,128)(2,1)S(1)}, u32[]{:S(2)}, u32[]{:S(2)}) collective-permute-start(bf16[2,192,1152]{2,1,0:T(8,128)(2,1)S(1)} %add_convert_fusion.1), channel_id=1, source_target_pairs={{0,8},{4,20},{8,0},{12,28},{16,24},{20,4},{24,16},{28,12},{1,9},{5... | collective-permute-start | bytes 2654216 | tf_op jit(solution)/shard_map/ppermute | solution.py:857
  212.9 44.7 %collective-permute-start.25 = (bf16[2,512,384]{2,1,0:T(8,128)(2,1)S(1)}, bf16[2,512,384]{2,1,0:T(8,128)(2,1)S(1)}, u32[]{:S(2)}, u32[]{:S(2)}) collective-permute-start(bf16[2,512,384]{2,1,0:T(8,128)(2,1)S(1)} %copy-done.41), channel_id=1, source_target_pairs={{0,1},{1,0},{2,3},{3,2},{4,5},{5,4},{6,7},{7,6},{8,9},{9,8},{10,11... | collective-permute-start | bytes 2359304 | tf_op jit(solution)/shard_map/ppermute | solution.py:864
  221.8 33.9 %collective-permute-start.22 = (f32[8,1536]{1,0:T(8,128)S(1)}, f32[8,1536]{1,0:T(8,128)S(1)}, u32[]{:S(2)}, u32[]{:S(2)}) collective-permute-start(f32[8,1536]{1,0:T(8,128)S(1)} %slice_select_fusion.t0_ref.refs_0_), channel_id=1, source_target_pairs={{0,1},{1,0},{2,3},{3,2},{4,5},{5,4},{6,7},{7,6},{8,9},{9,8},{10,11... | collective-permute-start | bytes 147464 | tf_op jit(solution)/shard_map/ppermute | solution.py:833
  223.3 36.2 %collective-permute-start.23 = (f32[8,1536]{1,0:T(8,128)S(1)}, f32[8,1536]{1,0:T(8,128)S(1)}, u32[]{:S(2)}, u32[]{:S(2)}) collective-permute-start(f32[8,1536]{1,0:T(8,128)S(1)} %slice_select_fusion.t0_ref.refs_0_), channel_id=1, source_target_pairs={{0,2},{1,3},{2,0},{3,1},{4,6},{5,7},{6,4},{7,5},{8,10},{9,11},{10,... | collective-permute-start | bytes 147464 | tf_op jit(solution)/shard_map/ppermute | solution.py:833
  227.5 34.0 %collective-permute-start.36 = (bf16[1,192,1152]{2,1,0:T(8,128)(2,1)S(1)}, bf16[1,192,1152]{2,1,0:T(8,128)(2,1)S(1)}, u32[]{:S(2)}, u32[]{:S(2)}) collective-permute-start(bf16[1,192,1152]{2,1,0:T(8,128)(2,1)S(1)} %constant_dynamic-slice_fusion), channel_id=1, source_target_pairs={{0,4},{4,0},{1,5},{5,1},{2,6},{6,2},{3,7},{7,3},{8,12},{12,8},{9,1... | collective-permute-start | bytes 1327112 | tf_op jit(solution)/shard_map/ppermute | solution.py:858
  239.7 22.9 %collective-permute-start.32 = (bf16[1,192,1536]{2,1,0:T(8,128)(2,1)S(1)}, bf16[1,192,1536]{2,1,0:T(8,128)(2,1)}, u32[]{:S(2)}, u32[]{:S(2)}) collective-permute-start(bf16[1,192,1536]{2,1,0:T(8,128)(2,1)S(1)} %constant_dynamic-slice_fusion.1), channel_id=1, source_target_pairs={{0,4},{4,0},{1,5},{5,1},{2,6},{6,2},{3,7},{7,3},{8,12},{12,8},{9,1... | collective-permute-start | bytes 1769480 | tf_op jit(solution)/shard_map/ppermute | solution.py:858
  255.7 72.0 %collective-permute-start.16 = (bf16[1,512,384]{2,1,0:T(8,128)(2,1)}, bf16[1,512,384]{2,1,0:T(8,128)(2,1)S(1)}, u32[]{:S(2)}, u32[]{:S(2)}) collective-permute-start(bf16[1,512,384]{2,1,0:T(8,128)(2,1)} %add_convert_fusion.6), channel_id=1, source_target_pairs={{0,2},{1,3},{2,0},{3,1},{4,6},{5,7},{6,4},{7,5},{8,10},{9,11},{10,... | collective-permute-start | bytes 1179656 | tf_op jit(solution)/shard_map/ppermute | solution.py:865
  257.6 71.2 %collective-permute-start.14 = (bf16[1,512,384]{2,1,0:T(8,128)(2,1)}, bf16[1,512,384]{2,1,0:T(8,128)(2,1)S(1)}, u32[]{:S(2)}, u32[]{:S(2)}) collective-permute-start(bf16[1,512,384]{2,1,0:T(8,128)(2,1)} %add_convert_fusion.7), channel_id=1, source_target_pairs={{0,2},{1,3},{2,0},{3,1},{4,6},{5,7},{6,4},{7,5},{8,10},{9,11},{10,... | collective-permute-start | bytes 1179656 | tf_op jit(solution)/shard_map/ppermute | solution.py:865
  259.5 81.4 %collective-permute-start.28 = (bf16[1,512,384]{2,1,0:T(8,128)(2,1)}, bf16[1,512,384]{2,1,0:T(8,128)(2,1)}, u32[]{:S(2)}, u32[]{:S(2)}) collective-permute-start(bf16[1,512,384]{2,1,0:T(8,128)(2,1)} %add_convert_fusion.4), channel_id=1, source_target_pairs={{0,2},{1,3},{2,0},{3,1},{4,6},{5,7},{6,4},{7,5},{8,10},{9,11},{10,... | collective-permute-start | bytes 1179656 | tf_op jit(solution)/shard_map/ppermute | solution.py:865
  261.5 79.4 %collective-permute-start.26 = (bf16[1,512,384]{2,1,0:T(8,128)(2,1)}, bf16[1,512,384]{2,1,0:T(8,128)(2,1)}, u32[]{:S(2)}, u32[]{:S(2)}) collective-permute-start(bf16[1,512,384]{2,1,0:T(8,128)(2,1)} %add_convert_fusion.5), channel_id=1, source_target_pairs={{0,2},{1,3},{2,0},{3,1},{4,6},{5,7},{6,4},{7,5},{8,10},{9,11},{10,... | collective-permute-start | bytes 1179656 | tf_op jit(solution)/shard_map/ppermute | solution.py:865
  262.6 30.8 %collective-permute-start.24 = (f32[8,1536]{1,0:T(8,128)S(1)}, f32[8,1536]{1,0:T(8,128)S(1)}, u32[]{:S(2)}, u32[]{:S(2)}) collective-permute-start(f32[8,1536]{1,0:T(8,128)S(1)} %slice_select_fusion.t0_ref.refs_0_), channel_id=1, source_target_pairs={{0,3},{1,2},{2,1},{3,0},{4,7},{5,6},{6,5},{7,4},{8,11},{9,10},{10,... | collective-permute-start | bytes 147464 | tf_op jit(solution)/shard_map/ppermute | solution.py:833
  293.4 51.9 %collective-permute-start.37 = (bf16[192,256]{1,0:T(8,128)(2,1)}, bf16[192,256]{1,0:T(8,128)(2,1)}, u32[]{:S(2)}, u32[]{:S(2)}) collective-permute-start(bf16[192,256]{1,0:T(8,128)(2,1)} %get-tuple-element.116), channel_id=1, source_target_pairs={{0,1},{1,0},{2,3},{3,2},{4,5},{5,4},{6,7},{7,6},{8,9},{9,8},{10,11... | collective-permute-start | bytes 294920 | tf_op jit(solution)/shard_map/ppermute | solution.py:833
  327.6 17.6 %collective-permute-start.38 = (bf16[192,256]{1,0:T(8,128)(2,1)}, bf16[192,256]{1,0:T(8,128)(2,1)}, u32[]{:S(2)}, u32[]{:S(2)}) collective-permute-start(bf16[192,256]{1,0:T(8,128)(2,1)} %get-tuple-element.116), channel_id=1, source_target_pairs={{0,2},{1,3},{2,0},{3,1},{4,6},{5,7},{6,4},{7,5},{8,10},{9,11},{10,... | collective-permute-start | bytes 294920 | tf_op jit(solution)/shard_map/ppermute | solution.py:833
  (72 other events, 1222.6 us)

commit v2 on v1

--- a/solution.py
+++ b/solution.py
@@ -20,7 +20,8 @@
 LEAD = SHARED + LANES
 BF = jnp.bfloat16
 F32 = jnp.float32
-LIMITS = {"k_final": 60, "k_tokens": 60, "k_sums": 60}
+OUT_FIRST = 1
+LIMITS = {"k_output": 60, "k_final": 60, "k_tokens0": 60, "k_tokens1": 60, "k_sums": 60, "k_packin": 60}
 
 
 def dot_nn(a, b):
@@ -335,8 +336,7 @@
         hist_ref[pl.ds(k + 1, 1)] = hold[...].astype(BF)[None]
 
 
-def store_halves(outs, *refs):
-    first = pl.program_id(0) < pl.num_programs(0) // 2
+def store_parts(outs, first, *refs):
     for here, keep_ref, send_ref in ((first, *refs[:2]), (~first, *refs[2:])):
 
         @pl.when(here)
@@ -383,7 +383,7 @@
     square = exact(dot_nt, ones, square, 3, False)
     cross = exact(dot_nt, ones, cross, 3, False)
     stat_ref[...] = jnp.where(iota((8, STRETCH), 0) == 0, square, cross)
-    store_halves(outs, keepa_ref, senda_ref, keepb_ref, sendb_ref)
+    store_parts(outs, k < OUT_FIRST, keepa_ref, senda_ref, keepb_ref, sendb_ref)
 
 
 def padded(v):
@@ -453,16 +453,14 @@
 def conv_back(post, u, taps, masks, kgrad_ref, lanes):
     full = post.shape[0] + HALO
     pad = jnp.zeros((HALO, post.shape[1]), F32)
-    total = jnp.concatenate([pad, post * taps[3:4]], axis=0)
+    total = jnp.concatenate([pad, post], axis=0) * taps[3:4]
     kgrad_ref[4:5, lanes] += jnp.sum(post, axis=0, keepdims=True)
     kgrad_ref[3:4, lanes] += jnp.sum(post * u[HALO:], axis=0, keepdims=True)
     for j in (1, 2, 3):
-        here = post * masks[j - 1]
-        kgrad_ref[3 - j : 4 - j, lanes] += jnp.sum(
-            here * pltpu.roll(u, j, 0)[HALO:], axis=0, keepdims=True
-        )
-        wide = jnp.concatenate([pad, here * taps[3 - j : 4 - j]], axis=0)
-        total = total + pltpu.roll(wide, full - j, 0)
+        wide = jnp.concatenate([pad, post * masks[j - 1]], axis=0)
+        moved = pltpu.roll(wide, full - j, 0)
+        kgrad_ref[3 - j : 4 - j, lanes] += jnp.sum(moved * u, axis=0, keepdims=True)
+        total = total + moved * taps[3 - j : 4 - j]
     return total
 
 
@@ -639,7 +637,8 @@
             cross = cross + inner[:, part : part + LANES]
     row = exact(dot_nt, jnp.ones((8, LANES), BF), cross, 3, False)[0:1]
     cross_ref[2:3, pl.ds(pl.multiple_of(i * rows, LANES), rows)] = row
-    store_halves(outs, keepa_ref, senda_ref, keepb_ref, sendb_ref)
+    first = i < pl.num_programs(0) // 2
+    store_parts(outs, first, keepa_ref, senda_ref, keepb_ref, sendb_ref)
 
 
 def put_chunk(idx_ref, keep_ref, send_ref, lanes, value):
@@ -681,6 +680,16 @@
     ]
     value = dot_tn(jnp.concatenate(scaled, axis=1), gg_ref[...])
     put_chunk(idx_ref, keep_ref, send_ref, slice(wide, wide + channels), value)
+
+
+def add_kernel(a_ref, b_ref, out_ref):
+    out_ref[...] = (a_ref[...].astype(F32) + b_ref[...].astype(F32)).astype(BF)
+
+
+def near_kernel(idx_ref, keep_ref, got_ref, far_ref, out_ref):
+    for h in (0, 1):
+        total = keep_ref[h].astype(F32) + got_ref[h].astype(F32)
+        out_ref[h] = (total + jnp.where(idx_ref[4] == h, far_ref[0].astype(F32), 0.0)).astype(BF)
 
 
 def final_kernel(idx_ref, *refs):
@@ -723,40 +732,36 @@
 def output_kernel(own_ref, inv_ref, *refs):
     out_ref = refs[-1]
     inv = inv_ref[...]
-    for part, (keep_ref, got_ref, far_ref) in enumerate((refs[0:3], refs[3:6])):
-
-        @pl.when(pl.program_id(0) == part)
+    first = pl.program_id(0) < OUT_FIRST
+    for here, terms in ((first, refs[0:3]), (~first, refs[3:6])):
+
+        @pl.when(here)
         def _():
             for at in range(0, out_ref.shape[1], LANES):
                 lanes = slice(at, at + LANES)
-                total = keep_ref[0, :, lanes].astype(F32) + got_ref[0, :, lanes].astype(F32)
-                total = (total + far_ref[0, :, lanes].astype(F32)) * inv
+                total = terms[0][0, :, lanes].astype(F32) + terms[1][0, :, lanes].astype(F32)
+                total = (total + terms[2][0, :, lanes].astype(F32)) * inv
                 out_ref[:, lanes] = (own_ref[:, lanes].astype(F32) + total).astype(BF)
 
 
 def tokens_kernel(
-    width, own_ref, cot_ref, inv_ref, t0_ref, t1_ref, t2_ref, t3_ref, gain_ref,
-    keepa_ref, gota_ref, fara_ref, keepb_ref, gotb_ref, farb_ref, out_ref,
+    width, own_ref, cot_ref, inv_ref, t0_ref, t1_ref, t2_ref, t3_ref, gain_ref, keep_ref, got_ref, far_ref, *refs
 ):
+    out_ref = refs[-1]
     inv = inv_ref[...]
     pick = (iota((8, LANES), 0) == 2).astype(F32).astype(BF)
     cross = (t0_ref[...] + t1_ref[...]) + (t2_ref[...] + t3_ref[...])
     cross = exact(dot_tn, cross, pick, 3, True)
     back = inv * inv * (cross / width)
-    halves = ((keepa_ref, gota_ref, fara_ref), (keepb_ref, gotb_ref, farb_ref))
-    for part, (keep_ref, got_ref, far_ref) in enumerate(halves):
-
-        @pl.when(pl.program_id(0) == part)
-        def _():
-            for at in range(0, out_ref.shape[1], LANES):
-                lanes = slice(at, at + LANES)
-                total = keep_ref[0, :, lanes].astype(F32) + got_ref[0, :, lanes].astype(F32)
-                total = total + far_ref[0, :, lanes].astype(F32)
-                out_ref[:, lanes] = (
-                    inv * gain_ref[0:1, lanes] * total
-                    - own_ref[:, lanes].astype(F32) * back
-                    + cot_ref[:, lanes].astype(F32)
-                )
+    for at in range(0, out_ref.shape[1], LANES):
+        lanes = slice(at, at + LANES)
+        total = keep_ref[0, :, lanes].astype(F32) + got_ref[0, :, lanes].astype(F32)
+        total = total + far_ref[0, :, lanes].astype(F32)
+        out_ref[:, lanes] = (
+            inv * gain_ref[0:1, lanes] * total
+            - own_ref[:, lanes].astype(F32) * back
+            + cot_ref[:, lanes].astype(F32)
+        )
 
 
 def whole(array):
@@ -764,11 +769,12 @@
     return pl.BlockSpec(array.shape, lambda *_: (0,) * rank)
 
 
-def call(name, kernel, grid, ins, in_specs, outs, out_specs, scratch=(), flops=0, prefetch=0):
+def call(name, kernel, grid, ins, in_specs, outs, out_specs, scratch=(), flops=0, prefetch=0, alias={}):
     moved = sum(a.size * a.dtype.itemsize for a in (*ins, *outs))
     return pl.pallas_call(
         kernel,
         out_shape=outs,
+        input_output_aliases=alias,
         grid_spec=pltpu.PrefetchScalarGridSpec(
             num_scalar_prefetch=prefetch,
             grid=grid,
@@ -787,10 +793,6 @@
 
 def shape(dims, kind):
     return jax.ShapeDtypeStruct(dims, kind)
-
-
-def add(*terms):
-    return sum(term.astype(F32) for term in terms).astype(BF)
 
 
 def per_device(
@@ -849,20 +851,30 @@
             shard, near.reshape(chunk, columns), near_other.reshape(chunk, columns), far[0], far_other[0]
         )
 
-    def scatter_rows(keep, send):
+    def add_block(name, a, b, at):
+        dims = (1, *a.shape[1:])
+        spec = pl.BlockSpec(dims, lambda i: (at, 0, 0))
+        out = pl.BlockSpec(dims, lambda i: (0, 0, 0))
+        return call(name, add_kernel, (1,), (a, b), [spec, spec], (shape(dims, BF),), [out])[0]
+
+    def scatter_rows(name, keep, send):
         got = lax.ppermute(send, "ctx", swap)
-        far = lax.ppermute(add(keep[2:3], got[2:3]), both, turn)
-        which = iota((2, 1, 1), 0) == c
-        near = add(keep[0:2], got[0:2], jnp.where(which, far.astype(F32), 0.0))
+        far = lax.ppermute(add_block(f"k_{name}2", keep, got, 2), both, turn)
+        columns = keep.shape[2]
+        two = pl.BlockSpec((2, half, columns), lambda i, *_: (0, 0, 0))
+        outs = (shape((2, half, columns), BF),)
+        near = call(
+            f"k_{name}3", near_kernel, (1,), (idx, keep, got, far), [two, two, whole(far)], outs, [two], prefetch=1
+        )[0]
         near = lax.ppermute(near, both, role)
         return keep, got, near, lax.ppermute(one(near, 1 - c), "ctx", swap)
 
-    def scatter_tp(keep, send):
+    def scatter_tp(name, keep, send):
         if not line:
             full = jnp.concatenate([keep[0], send[0], keep[1], send[1]], axis=1)
             return (lax.psum_scatter(full, "tp", scatter_dimension=1, tiled=True),)
         got = lax.ppermute(send, "tp", [(i, i ^ 1) for i in range(nt)])
-        far = lax.ppermute(add(keep[1:2], got[1:2]), "tp", [(i, i ^ 2) for i in range(nt)])
+        far = lax.ppermute(add_block(f"k_{name}", keep, got, 1), "tp", [(i, i ^ 2) for i in range(nt)])
         return keep, got, far
 
     any_spec = pl.BlockSpec(memory_space=pl.ANY)
@@ -964,19 +976,21 @@
     )
 
     outs = (
-        shape((length, channels), BF), shape((length, channels), BF), *(shape((2, mid, chunk), BF),) * 4,
+        shape((length, channels), BF), shape((length, channels), BF), *(shape((2, OUT_FIRST * STRETCH, chunk), BF),) * 2,
+        *(shape((2, length - OUT_FIRST * STRETCH, chunk), BF),) * 2,
         shape((8, length), F32),
     )
+    out_a = pl.BlockSpec((2, STRETCH, chunk), lambda i, *_: (0, jnp.minimum(i, OUT_FIRST - 1), 0))
+    out_b = pl.BlockSpec((2, STRETCH, chunk), lambda i, *_: (0, jnp.maximum(i - OUT_FIRST, 0), 0))
     ins = (idx, *w_go, normed, y, cot2, gate_row)
     gate, gg, *out_parts, stat = call(
         "k_gate", gate_kernel, (nb,), ins,
         [any_spec] * 5 + [block(width), block(channels), block(width), whole(gate_row)],
-        outs, [block(channels)] * 2 + [part_a, part_a, part_b, part_b, across()],
+        outs, [block(channels)] * 2 + [out_a, out_a, out_b, out_b, across()],
         scratch=[pltpu.VMEM((nf, chunk, 2 * wide), BF), sems],
         prefetch=1, flops=4 * length * width * channels,
     )
-    out_a = scatter_tp(*out_parts[:2])
-    out_b = scatter_tp(*out_parts[2:])
+    out_terms = (*scatter_tp("roa", *out_parts[:2]), *scatter_tp("rob", *out_parts[2:]))
     stat = tp_sum(stat)
     outs = (shape((length, channels), BF),)
     gng = call(
@@ -1012,7 +1026,7 @@
         outs, [whole(outs[0])] * 2, prefetch=1,
         flops=4 * length * width * channels,
     )
-    grad_go = scatter_rows(*grad_go)
+    grad_go = scatter_rows("go", *grad_go)
 
     outs = (
         shape((length, lead), BF), shape((HALO, lead), BF), shape((16, width), F32), shape((HALO, width), F32),
@@ -1052,8 +1066,8 @@
         scratch=[pltpu.VMEM((nf, chunk, wide), BF), held_in, sems, sems],
         prefetch=1, flops=2 * length * width * (lead + channels),
     )
-    normed_a = scatter_tp(keep_a, send_a)
-    normed_b = scatter_tp(keep_b, send_b)
+    normed_a = scatter_tp("rna", keep_a, send_a)
+    normed_b = scatter_tp("rnb", keep_b, send_b)
 
     outs = (shape((4, half, lead), BF),) * 2
     grad_w = call(
@@ -1065,7 +1079,7 @@
         outs, [whole(outs[0])] * 2, prefetch=1,
         flops=2 * length * width * lead,
     )
-    grad_w = scatter_rows(*grad_w)
+    grad_w = scatter_rows("w", *grad_w)
 
     sums = sums + lax.ppermute(sums, "ctx", swap)
     for m in (1, 2):
@@ -1105,26 +1119,34 @@
     outs = (shape((length, share), BF),)
     if line:
         spec = pl.BlockSpec((mid, share), lambda i: (i, 0))
-        only = pl.BlockSpec((1, mid, share), lambda i: (0, 0, 0))
-        inv_spec = pl.BlockSpec((mid, LANES), lambda i: (i, 0))
+        term_a = pl.BlockSpec((1, STRETCH, share), lambda i: (0, jnp.minimum(i, OUT_FIRST - 1), 0))
+        term_b = pl.BlockSpec((1, STRETCH, share), lambda i: (0, jnp.maximum(i - OUT_FIRST, 0), 0))
         output = call(
-            "k_output", output_kernel, (2,), (own_tokens, inv_gate, *out_a, *out_b), [spec, inv_spec] + [only] * 6,
-            outs, [spec],
+            "k_output", output_kernel, (nb,), (own_tokens, inv_gate, *out_terms),
+            [block(share), block(LANES)] + [term_a] * 3 + [term_b] * 3,
+            outs, [block(share)],
         )[0]
         outs = (shape((length, share), F32),)
         gain2 = own_gain[None]
-        grad_tokens = call(
-            "k_tokens", functools.partial(tokens_kernel, width), (2,),
-            (own_tokens, own_cot, inv_rms, *sum_terms, gain2, *normed_a, *normed_b),
-            [spec, spec, inv_spec]
-            + [pl.BlockSpec((8, mid), lambda i: (0, i))] * 4
-            + [whole(gain2)]
-            + [only] * 6,
-            outs, [spec],
-        )[0]
+        grad_tokens = ()
+        for part, terms in enumerate((normed_a, normed_b)):
+            at = part * (mid // STRETCH)
+            grad_tokens = call(
+                f"k_tokens{part}", functools.partial(tokens_kernel, width), (mid // STRETCH,),
+                (own_tokens, own_cot, inv_rms, *sum_terms, gain2, *terms, *grad_tokens),
+                [pl.BlockSpec((STRETCH, share), lambda i, at=at: (i + at, 0))] * 2
+                + [pl.BlockSpec((STRETCH, LANES), lambda i, at=at: (i + at, 0))]
+                + [pl.BlockSpec((8, STRETCH), lambda i, at=at: (0, i + at))] * 4
+                + [whole(gain2)]
+                + [pl.BlockSpec((1, STRETCH, share), lambda i: (0, i, 0))] * 3
+                + [any_spec] * part,
+                outs, [pl.BlockSpec((STRETCH, share), lambda i, at=at: (i + at, 0))],
+                alias={11: 0} if part else {},
+            )
+        grad_tokens = grad_tokens[0]
     else:
         normed_sum = jnp.concatenate([normed_a[0], normed_b[0]], axis=0).astype(F32)
-        out_sum = jnp.concatenate([out_a[0], out_b[0]], axis=0).astype(F32)
+        out_sum = jnp.concatenate(out_terms, axis=0).astype(F32)
         output = (own_tokens.astype(F32) + inv_gate[:, :1] * out_sum).astype(BF)
         inv = inv_rms[:, :1]
         grad_tokens = (

time: 348 us -> 316 us (0.908)
  starting transfers between devices: 85.2 us -> 63.5 us
  other arithmetic: 12.8 us -> 2.13 us
  Pallas kernels: 120 us -> 128 us
  local copies, waits for them, and re-layouts: 23.3 us -> 16.1 us
    ppermute x4, waiting for transfers between devices: 18.8 us -> 46.1 us  [scatter_tp(): got = lax.ppermute(send, 'tp', [(i, i ^ 1) for i in range(nt)])]
    ppermute x6, starting transfers between devices: 44.7 us -> 23.9 us  [tp_terms(): lax.ppermute(v, 'tp', [(i, i ^ m) for i in range(nt)])]
    ppermute x6, waiting for transfers between devices: 37.6 us -> 18.9 us  [tp_terms(): lax.ppermute(v, 'tp', [(i, i ^ m) for i in range(nt)])]
    ppermute x6, waiting for transfers between devices: 13.2 us -> 3.71 us  [the longest x2 3.7 us: scatter_rows(): far = lax.ppermute(add_block(f'k_{name}2', keep, got, 2), both, turn)]
    convert_element_type x8 -> x0, other arithmetic: 9.49 us -> none  [add(): return sum((term.astype(F32) for term in terms)).astype(BF)]
    unnamed x112 -> x102, local copies, waits for them, and re-layouts: 16.7 us -> 7.44 us
    pallas_call x16 -> x25, Pallas kernels: 120 us -> 128 us  [call(): pl.pallas_call(kernel, out_shape=outs, input_output_aliases=alias, grid_s...]
  transfers between devices with their start and end apart: 40 -> 40, of which waited for: 15 -> 16; matrix products, arithmetic and copies ran while one was open for 5% -> 3% of each run, Pallas kernels for 29% -> 34%
where the time goes in v2:
time: 316 us
  Pallas kernels  128 us (41%)
  waiting for transfers between devices  104 us (33%)
  starting transfers between devices  63.5 us (20%)
  local copies, waits for them, and re-layouts  16.1 us (5%)
    pallas_call x25, Pallas kernels, call(): pl.pallas_call(kernel, out_shape=outs, input_output_aliases=alias, grid_s...  128 us
    ppermute x4, waiting for transfers between devices, scatter_tp(): got = lax.ppermute(send, 'tp', [(i, i ^ 1) for i in range(nt)])  46.1 us
    ppermute x6, starting transfers between devices, tp_terms(): lax.ppermute(v, 'tp', [(i, i ^ m) for i in range(nt)])  23.9 us
    ppermute x2, waiting for transfers between devices, gather_rows(): near = lax.ppermute(pieces, both, role)  23.4 us
    ppermute x6, waiting for transfers between devices, tp_terms(): lax.ppermute(v, 'tp', [(i, i ^ m) for i in range(nt)])  18.9 us
    unnamed x102, local copies, waits for them, and re-layouts  7.44 us
    ppermute x2, waiting for transfers between devices, per_device(): sums = sums + lax.ppermute(sums, 'fsdp', [(i, i ^ m) for i in range(nf)])  6.91 us
    ppermute x4, starting transfers between devices, scatter_tp(): lax.ppermute(add_block(f'k_{name}', keep, got, 1), 'tp', [(i, i ^ 2) for...  6.53 us
  transfers between devices with their start and end apart: 40, of which 16 were waited for; matrix products, arithmetic and copies ran while one was open for 3% of the time, Pallas kernels for 34%

profile of v2, /device:TPU:0, one launch (start us, length us, event | category | flops | bytes accessed | tf_op | source)
XLA Modules:
  0.0 315.6 jit_solution(2804724542684924868)
XLA Ops:
  2.8 3.0 collective-permute-start.5
  9.4 7.7 %collective-permute-done.5 = bf16[2,192,1152]{2,1,0:T(8,128)(2,1)} collective-permute-done((bf16[2,192,1152]{2,1,0:T(8,128)(2,1)}, bf16[2,192,1152]{2,1,0:T(8,128)(2,1)}, u32[]{:S(2)}, u32[]{:S(2)}) %collective-permute-start.5) | collective-permute-done | bytes 884768 | tf_op jit(solution)/shard_map/ppermute | solution.py:843
  23.7 15.7 %collective-permute-done.1 = bf16[2,192,1536]{2,1,0:T(8,128)(2,1)} collective-permute-done((bf16[2,192,1536]{2,1,0:T(8,128)(2,1)}, bf16[2,192,1536]{2,1,0:T(8,128)(2,1)}, u32[]{:S(2)}, u32[]{:S(2)}) %collective-permute-start.1) | collective-permute-done | bytes 1179680 | tf_op jit(solution)/shard_map/ppermute | solution.py:843
  49.0 16.9 %shard_map.206 = (bf16[1024,1152]{1,0:T(8,128)(2,1)S(1)}, bf16[16,1152]{1,0:T(8,128)(2,1)S(1)}, bf16[1024,768]{1,0:T(8,128)(2,1)S(1)}, bf16[1024,768]{1,0:T(8,12...) custom-call(s32[8]{0:T(128)S(1)} %stack.29.idx_ref, ...), custom_call_target="tpu_custom_call" | custom-call | flops 3825205248 | bytes 18391216 | tf_op jit(solution)/shard_map/pallas_call | solution.py:774
  69.1 6.2 %shard_map.207 = (f32[1024,768]{1,0:T(8,128)S(1)}, bf16[5,128,768]{2,1,0:T(8,128)(2,1)S(1)}) custom-call(bf16[1024,256]{1,0:T(8,128)(2,1)S(1)} %get-tuple-element.71.bc_ref, bf16[1024,768]{1,0:T(8,128)(2,1)S(1)} %get-tuple-element.72.x_ref, bf16[1024,768]{1,0:T(8,128)(2,1)S(1)} %get-tuple-element.73.xs_ref, f32[1024,128]{1,0:T(8,128)S(1)} %get-tuple-element.74.cum_ref, ...), custom_call_target="tpu_custom_call" | custom-call | flops 1610612736 | bytes 10223760 | tf_op jit(solution)/shard_map/pallas_call | solution.py:774
  75.3 14.3 %shard_map.208 = (bf16[1024,768]{1,0:T(8,128)(2,1)S(1)}, bf16[1024,768]{1,0:T(8,128)(2,1)S(1)}, bf16[2,256,384]{2,1,0:T(8,128)(2,1)S(1)}, bf16[2,256,384]{2,1,0:...) custom-call(s32[8]{0:T(128)S(1)} %stack.29.idx_ref, ...), custom_call_target="tpu_custom_call" | custom-call | flops 4831838208 | bytes 20483104 | tf_op jit(solution)/shard_map/pallas_call | solution.py:774
  92.0 2.6 collective-permute-start.11
  94.6 6.0 %shard_map.209.gng_ref = bf16[1024,768]{1,0:T(8,128)(2,1)S(1)} custom-call(s32[8]{0:T(128)S(1)} %stack.29.idx_ref, bf16[384,1536]{1,0:T(8,128)(2,1)} %shard_map.204.own_ref.own0_ref, bf16[384,1536]{1,0:T(8,128)(2,1)} %bitcast.10.near_ref.near0_ref, bf16[384,1536]{1,0:T(8,128)(2,1)} %bitcast.11.nearx_ref.nearx0_ref, ...), custom_call_target="tpu_custom_call" | custom-call | flops 2415919104 | bytes 9437216 | tf_op jit(solution)/shard_map/pallas_call | solution.py:774
  100.7 5.4 %shard_map.210 = (bf16[1024,768]{1,0:T(8,128)(2,1)S(1)}, bf16[1024,768]{1,0:T(8,128)(2,1)S(1)}, f32[1024,128]{1,0:T(8,128)S(1)}, bf16[128,768]{1,0:T(8,128)(2,1)S(1)}, f32[8,768]{1,0:T(8,128)S(1)}) custom-call(f32[8,1024]{1,0:T(8,128)S(1)} %add_add_fusion.1.stat_ref, f32[1024,768]{1,0:T(8,128)S(1)} %get-tuple-element.78.y_ref, ...), custom_call_target="tpu_custom_call" | custom-call | flops 201326592 | bytes 11398144 | tf_op jit(solution)/shard_map/pallas_call | solution.py:774
  107.6 10.2 %shard_map.221 = (bf16[4,192,1536]{2,1,0:T(8,128)(2,1)S(1)}, bf16[4,192,1536]{2,1,0:T(8,128)(2,1)S(1)}) custom-call(s32[8]{0:T(128)S(1)} %stack.29.idx_ref, bf16[1024,1536]{1,0:T(8,128)(2,1)S(1)} %get-tuple-element.68.normed_ref, bf16[1024,768]{1,0:T(8,128)(2,1)S(1)} %get-tuple-element.88.gi_ref, bf16[1024,1536]{1,0:T(8,128)(2,1)S(1)} %bitcast.28, ...), custom_call_target="tpu_custom_call" | custom-call | flops 4831838208 | bytes 14680096 | tf_op jit(solution)/shard_map/pallas_call | solution.py:774
  119.1 21.1 %shard_map.214 = (bf16[1024,1152]{1,0:T(8,128)(2,1)S(1)}, bf16[16,1152]{1,0:T(8,128)(2,1)S(1)}, f32[16,1536]{1,0:T(8,128)S(1)}, f32[16,1536]{1,0:T(8,128)S(1)}) custom-call(s32[8]{0:T(128)S(1)} %stack.29.idx_ref, bf16[384,1152]{1,0:T(8,128)(2,1)S(1)} %copy-done.11, bf16[384,1152]{1,0:T(8,128)(2,1)} %bitcast.16.near_ref, ...), custom_call_target="tpu_custom_call" | custom-call | flops 3221225472 | bytes 25284784 | tf_op jit(solution)/shard_map/pallas_call | solution.py:774
  140.2 7.3 %shard_map.224 = (bf16[4,192,1152]{2,1,0:T(8,128)(2,1)S(1)}, bf16[4,192,1152]{2,1,0:T(8,128)(2,1)S(1)}) custom-call(s32[8]{0:T(128)S(1)} %stack.29.idx_ref, bf16[1024,1536]{1,0:T(8,128)(2,1)S(1)} %get-tuple-element.68.normed_ref, bf16[16,1536]{1,0:T(8,128)(2,1)S(1)} %get-tuple-element.69.nhalo_ref, bf16[1024,1152]{1,0:T(8,128)(2,1)S(1)} %get-tuple-element.99.g_ref, ...), custom_call_target="tpu_custom_call" | custom-call | flops 3623878656 | bytes 9130016 | tf_op jit(solution)/shard_map/pallas_call | solution.py:774
  166.3 13.9 %shard_map.215 = (bf16[2,512,384]{2,1,0:T(8,128)(2,1)S(1)}, bf16[2,512,384]{2,1,0:T(8,128)(2,1)S(1)}, bf16[2,512,384]{2,1,0:T(8,128)(2,1)S(1)}, bf16[2,512,384]{...) custom-call(s32[8]{0:T(128)S(1)} %stack.29.idx_ref, ...), custom_call_target="tpu_custom_call" | custom-call | flops 6039797760 | bytes 18825248 | tf_op jit(solution)/shard_map/pallas_call | solution.py:774
  183.4 4.5 %collective-permute-done.20 = f32[16,1536]{1,0:T(8,128)S(1)} collective-permute-done((f32[16,1536]{1,0:T(8,128)S(1)}, f32[16,1536]{1,0:T(8,128)S(1)}, u32[]{:S(2)}, u32[]{:S(2)}) %collective-permute-start.20) | collective-permute-done | bytes 98336 | tf_op jit(solution)/shard_map/ppermute | solution.py:1086
  200.5 13.9 %collective-permute-done.13.b_ref.refs_1_ = bf16[2,256,384]{2,1,0:T(8,128)(2,1)S(1)} collective-permute-done((bf16[2,256,384]{2,1,0:T(8,128)(2,1)}, bf16[2,256,384]{2,1,0:T(8,128)(2,1)S(1)}, u32[]{:S(2)}, u32[]{:S(2)}) %collective-permute-start.13) | collective-permute-done | bytes 393248 | tf_op jit(solution)/shard_map/ppermute | solution.py:876
  214.5 16.8 %collective-permute-done.27.b_ref.got_ref = bf16[2,512,384]{2,1,0:T(8,128)(2,1)S(1)} collective-permute-done((bf16[2,512,384]{2,1,0:T(8,128)(2,1)}, bf16[2,512,384]{2,1,0:T(8,128)(2,1)S(1)}, u32[]{:S(2)}, u32[]{:S(2)}) %collective-permute-start.27) | collective-permute-done | bytes 786464 | tf_op jit(solution)/shard_map/ppermute | solution.py:876
  231.3 15.5 %collective-permute-done.25.b_ref.got_ref = bf16[2,512,384]{2,1,0:T(8,128)(2,1)S(1)} collective-permute-done((bf16[2,512,384]{2,1,0:T(8,128)(2,1)}, bf16[2,512,384]{2,1,0:T(8,128)(2,1)S(1)}, u32[]{:S(2)}, u32[]{:S(2)}) %collective-permute-start.25) | collective-permute-done | bytes 786464 | tf_op jit(solution)/shard_map/ppermute | solution.py:876
  250.0 18.1 %collective-permute-done.23.t2_ref.refs_2_ = f32[8,1536]{1,0:T(8,128)S(1)} collective-permute-done((f32[8,1536]{1,0:T(8,128)S(1)}, f32[8,1536]{1,0:T(8,128)S(1)}, u32[]{:S(2)}, u32[]{:S(2)}) %collective-permute-start.23) | collective-permute-done | bytes 49184 | tf_op jit(solution)/shard_map/ppermute | solution.py:835
  268.2 3.0 collective-permute-start.14
  272.8 4.5 %shard_map.227 = (f32[2,192,768]{2,1,0:T(8,128)}, f32[12,192]{1,0:T(8,128)}, bf16[192,256]{1,0:T(8,128)(2,1)}, f32[192,768]{1,0:T(8,128)}) custom-call(s32[8]{0:T(128)} %copy-done.28, bf16[4,192,1536]{2,1,0:T(8,128)(2,1)} %copy-done, bf16[4,192,1536]{2,1,0:T(8,128)(2,1)} %copy-done.1, bf16[2,192,1536]{2,1,0:T(8,128)(2,1)} %collective-permute-done.31.refs_2_, ...), custom_call_target="tpu_custom_call" | custom-call | bytes 13231136 | tf_op jit(solution)/shard_map/pallas_call | solution.py:774
  278.1 17.5 %collective-permute-start.37 = (bf16[192,256]{1,0:T(8,128)(2,1)}, bf16[192,256]{1,0:T(8,128)(2,1)S(1)}, u32[]{:S(2)}, u32[]{:S(2)}) collective-permute-start(bf16[192,256]{1,0:T(8,128)(2,1)} %get-tuple-element.116), channel_id=1, source_target_pairs={{0,1},{1,0},{2,3},{3,2},{4,5},{5,4},{6,7},{7,6},{8,9},{9,8},{10,11... | collective-permute-start | bytes 294920 | tf_op jit(solution)/shard_map/ppermute | solution.py:835
  304.0 2.9 shard_map.218.refs_0_
  306.9 2.9 shard_map.219
  310.5 4.3 %shard_map.213 = bf16[1024,384]{1,0:T(8,128)(2,1)} custom-call(bf16[1024,384]{1,0:T(8,128)(2,1)} %copy-done.6, f32[1024,128]{1,0:T(8,128)} %copy-done.24, bf16[2,256,384]{2,1,0:T(8,128)(2,1)} %copy-done.20, bf16[2,256,384]{2,1,0:T(8,128)(2,1)} %copy-done.22, bf16[1,256,384]{2,1,0:T(8,128)(2,1)} %copy-done.47, bf16[2,768,384]{2,1,0:T(8,128)(2,1)} %copy-done.8, ...), custom_call_target="tpu_custom_call" | custom-call | bytes 6029312 | tf_op jit(solution)/shard_map/pallas_call | solution.py:774
  (202 shorter events, 80.3 us)
Async XLA Ops:
  9.4 29.9 %collective-permute-start.1 = (bf16[2,192,1536]{2,1,0:T(8,128)(2,1)}, bf16[2,192,1536]{2,1,0:T(8,128)(2,1)}, u32[]{:S(2)}, u32[]{:S(2)}) collective-permute-start(bf16[2,192,1536]{2,1,0:T(8,128)(2,1)} %bitcast.9), channel_id=1, source_target_pairs={{0,8},{4,20},{8,0},{12,28},{16,24},{20,4},{24,16},{28,12},{1,9},{5... | collective-permute-start | bytes 3538952 | tf_op jit(solution)/shard_map/ppermute | solution.py:843
  18.2 21.1 %collective-permute-start.7 = (bf16[1,192,1152]{2,1,0:T(8,128)(2,1)S(1)}, bf16[1,192,1152]{2,1,0:T(8,128)(2,1)}, u32[]{:S(2)}, u32[]{:S(2)}) collective-permute-start(bf16[1,192,1152]{2,1,0:T(8,128)(2,1)S(1)} %constant_dynamic-slice_fusion.2), channel_id=1, source_target_pairs={{0,16},{4,12},{8,24},{12,4},{16,0},{20,28},{24,8},{28,20},{1,17},{... | collective-permute-start | bytes 1327112 | tf_op jit(solution)/shard_map/ppermute | solution.py:847
  20.3 28.6 %collective-permute-start.6 = (bf16[2,192,1152]{2,1,0:T(8,128)(2,1)}, bf16[2,192,1152]{2,1,0:T(8,128)(2,1)}, u32[]{:S(2)}, u32[]{:S(2)}) collective-permute-start(bf16[2,192,1152]{2,1,0:T(8,128)(2,1)} %collective-permute-done.5), channel_id=1, source_target_pairs={{0,4},{4,0},{1,5},{5,1},{2,6},{6,2},{3,7},{7,3},{8,12},{12,8},{9,1... | collective-permute-start | bytes 2654216 | tf_op jit(solution)/shard_map/ppermute | solution.py:848
  22.2 26.4 %collective-permute-start.3 = (bf16[1,192,1536]{2,1,0:T(8,128)(2,1)}, bf16[1,192,1536]{2,1,0:T(8,128)(2,1)}, u32[]{:S(2)}, u32[]{:S(2)}) collective-permute-start(bf16[1,192,1536]{2,1,0:T(8,128)(2,1)} %constant_dynamic-slice_fusion.3), channel_id=1, source_target_pairs={{0,24},{4,28},{8,16},{12,20},{16,8},{20,12},{24,0},{28,4},{1,25},{... | collective-permute-start | bytes 1769480 | tf_op jit(solution)/shard_map/ppermute | solution.py:845
  39.3 36.0 %collective-permute-start.2 = (bf16[2,192,1536]{2,1,0:T(8,128)(2,1)}, bf16[2,192,1536]{2,1,0:T(8,128)(2,1)}, u32[]{:S(2)}, u32[]{:S(2)}) collective-permute-start(bf16[2,192,1536]{2,1,0:T(8,128)(2,1)} %collective-permute-done.1), channel_id=1, source_target_pairs={{0,4},{4,0},{1,5},{5,1},{2,6},{6,2},{3,7},{7,3},{8,12},{12,8},{9,1... | collective-permute-start | bytes 3538952 | tf_op jit(solution)/shard_map/ppermute | solution.py:848
  48.7 26.6 %collective-permute-start.4 = (bf16[1,192,1536]{2,1,0:T(8,128)(2,1)}, bf16[1,192,1536]{2,1,0:T(8,128)(2,1)S(1)}, u32[]{:S(2)}, u32[]{:S(2)}) collective-permute-start(bf16[1,192,1536]{2,1,0:T(8,128)(2,1)} %collective-permute-done.3), channel_id=1, source_target_pairs={{0,4},{4,0},{1,5},{5,1},{2,6},{6,2},{3,7},{7,3},{8,12},{12,8},{9,1... | collective-permute-start | bytes 1769480 | tf_op jit(solution)/shard_map/ppermute | solution.py:849
  117.9 29.8 %collective-permute-start.29 = (bf16[4,192,1536]{2,1,0:T(8,128)(2,1)S(1)}, bf16[4,192,1536]{2,1,0:T(8,128)(2,1)S(1)}, u32[]{:S(2)}, u32[]{:S(2)}) collective-permute-start(bf16[4,192,1536]{2,1,0:T(8,128)(2,1)S(1)} %get-tuple-element.111), channel_id=1, source_target_pairs={{0,4},{4,0},{1,5},{5,1},{2,6},{6,2},{3,7},{7,3},{8,12},{12,8},{9,1... | collective-permute-start | bytes 7077896 | tf_op jit(solution)/shard_map/ppermute | solution.py:861
  153.2 40.2 %collective-permute-start.15 = (bf16[2,768,384]{2,1,0:T(8,128)(2,1)}, bf16[2,768,384]{2,1,0:T(8,128)(2,1)S(1)}, u32[]{:S(2)}, u32[]{:S(2)}) collective-permute-start(bf16[2,768,384]{2,1,0:T(8,128)(2,1)} %get-tuple-element.85), channel_id=1, source_target_pairs={{0,1},{1,0},{2,3},{3,2},{4,5},{5,4},{6,7},{7,6},{8,9},{9,8},{10,11... | collective-permute-start | bytes 3538952 | tf_op jit(solution)/shard_map/ppermute | solution.py:876
  159.8 39.4 %collective-permute-start.31 = (bf16[2,192,1536]{2,1,0:T(8,128)(2,1)}, bf16[2,192,1536]{2,1,0:T(8,128)(2,1)}, u32[]{:S(2)}, u32[]{:S(2)}) collective-permute-start(bf16[2,192,1536]{2,1,0:T(8,128)(2,1)} %shard_map.223), channel_id=1, source_target_pairs={{0,8},{4,20},{8,0},{12,28},{16,24},{20,4},{24,16},{28,12},{1,9},{5... | collective-permute-start | bytes 3538952 | tf_op jit(solution)/shard_map/ppermute | solution.py:869
  164.6 31.2 %collective-permute-start.35 = (bf16[2,192,1152]{2,1,0:T(8,128)(2,1)}, bf16[2,192,1152]{2,1,0:T(8,128)(2,1)}, u32[]{:S(2)}, u32[]{:S(2)}) collective-permute-start(bf16[2,192,1152]{2,1,0:T(8,128)(2,1)} %shard_map.226), channel_id=1, source_target_pairs={{0,8},{4,20},{8,0},{12,28},{16,24},{20,4},{24,16},{28,12},{1,9},{5... | collective-permute-start | bytes 2654216 | tf_op jit(solution)/shard_map/ppermute | solution.py:869
  189.6 24.8 %collective-permute-start.13 = (bf16[2,256,384]{2,1,0:T(8,128)(2,1)}, bf16[2,256,384]{2,1,0:T(8,128)(2,1)S(1)}, u32[]{:S(2)}, u32[]{:S(2)}) collective-permute-start(bf16[2,256,384]{2,1,0:T(8,128)(2,1)} %copy-done.37), channel_id=1, source_target_pairs={{0,1},{1,0},{2,3},{3,2},{4,5},{5,4},{6,7},{7,6},{8,9},{9,8},{10,11... | collective-permute-start | bytes 1179656 | tf_op jit(solution)/shard_map/ppermute | solution.py:876
  192.7 38.6 %collective-permute-start.27 = (bf16[2,512,384]{2,1,0:T(8,128)(2,1)}, bf16[2,512,384]{2,1,0:T(8,128)(2,1)S(1)}, u32[]{:S(2)}, u32[]{:S(2)}) collective-permute-start(bf16[2,512,384]{2,1,0:T(8,128)(2,1)} %copy-done.36), channel_id=1, source_target_pairs={{0,1},{1,0},{2,3},{3,2},{4,5},{5,4},{6,7},{7,6},{8,9},{9,8},{10,11... | collective-permute-start | bytes 2359304 | tf_op jit(solution)/shard_map/ppermute | solution.py:876
  193.4 53.3 %collective-permute-start.25 = (bf16[2,512,384]{2,1,0:T(8,128)(2,1)}, bf16[2,512,384]{2,1,0:T(8,128)(2,1)S(1)}, u32[]{:S(2)}, u32[]{:S(2)}) collective-permute-start(bf16[2,512,384]{2,1,0:T(8,128)(2,1)} %copy-done.35), channel_id=1, source_target_pairs={{0,1},{1,0},{2,3},{3,2},{4,5},{5,4},{6,7},{7,6},{8,9},{9,8},{10,11... | collective-permute-start | bytes 2359304 | tf_op jit(solution)/shard_map/ppermute | solution.py:876
  195.8 114.1 %collective-permute-start.16 = (bf16[1,768,384]{2,1,0:T(8,128)(2,1)}, bf16[1,768,384]{2,1,0:T(8,128)(2,1)}, u32[]{:S(2)}, u32[]{:S(2)}) collective-permute-start(bf16[1,768,384]{2,1,0:T(8,128)(2,1)} %shard_map.212), channel_id=1, source_target_pairs={{0,2},{1,3},{2,0},{3,1},{4,6},{5,7},{6,4},{7,5},{8,10},{9,11},{10,... | collective-permute-start | bytes 1769480 | tf_op jit(solution)/shard_map/ppermute | solution.py:877
  199.3 68.9 %collective-permute-start.36 = (bf16[1,192,1152]{2,1,0:T(8,128)(2,1)S(1)}, bf16[1,192,1152]{2,1,0:T(8,128)(2,1)S(1)}, u32[]{:S(2)}, u32[]{:S(2)}) collective-permute-start(bf16[1,192,1152]{2,1,0:T(8,128)(2,1)S(1)} %constant_dynamic-slice_fusion), channel_id=1, source_target_pairs={{0,4},{4,0},{1,5},{5,1},{2,6},{6,2},{3,7},{7,3},{8,12},{12,8},{9,1... | collective-permute-start | bytes 1327112 | tf_op jit(solution)/shard_map/ppermute | solution.py:870
  214.4 56.7 %collective-permute-start.32 = (bf16[1,192,1536]{2,1,0:T(8,128)(2,1)S(1)}, bf16[1,192,1536]{2,1,0:T(8,128)(2,1)S(1)}, u32[]{:S(2)}, u32[]{:S(2)}) collective-permute-start(bf16[1,192,1536]{2,1,0:T(8,128)(2,1)S(1)} %constant_dynamic-slice_fusion.1), channel_id=1, source_target_pairs={{0,4},{4,0},{1,5},{5,1},{2,6},{6,2},{3,7},{7,3},{8,12},{12,8},{9,1... | collective-permute-start | bytes 1769480 | tf_op jit(solution)/shard_map/ppermute | solution.py:870
  231.3 17.5 %collective-permute-start.22 = (f32[8,1536]{1,0:T(8,128)S(1)}, f32[8,1536]{1,0:T(8,128)S(1)}, u32[]{:S(2)}, u32[]{:S(2)}) collective-permute-start(f32[8,1536]{1,0:T(8,128)S(1)} %slice_select_fusion.t0_ref.refs_0_), channel_id=1, source_target_pairs={{0,1},{1,0},{2,3},{3,2},{4,5},{5,4},{6,7},{7,6},{8,9},{9,8},{10,11... | collective-permute-start | bytes 147464 | tf_op jit(solution)/shard_map/ppermute | solution.py:835
  246.7 21.3 %collective-permute-start.23 = (f32[8,1536]{1,0:T(8,128)S(1)}, f32[8,1536]{1,0:T(8,128)S(1)}, u32[]{:S(2)}, u32[]{:S(2)}) collective-permute-start(f32[8,1536]{1,0:T(8,128)S(1)} %slice_select_fusion.t0_ref.refs_0_), channel_id=1, source_target_pairs={{0,2},{1,3},{2,0},{3,1},{4,6},{5,7},{6,4},{7,5},{8,10},{9,11},{10,... | collective-permute-start | bytes 147464 | tf_op jit(solution)/shard_map/ppermute | solution.py:835
  248.8 46.8 %collective-permute-start.28 = (bf16[1,512,384]{2,1,0:T(8,128)(2,1)S(1)}, bf16[1,512,384]{2,1,0:T(8,128)(2,1)S(1)}, u32[]{:S(2)}, u32[]{:S(2)}) collective-permute-start(bf16[1,512,384]{2,1,0:T(8,128)(2,1)S(1)} %shard_map.217), channel_id=1, source_target_pairs={{0,2},{1,3},{2,0},{3,1},{4,6},{5,7},{6,4},{7,5},{8,10},{9,11},{10,... | collective-permute-start | bytes 1179656 | tf_op jit(solution)/shard_map/ppermute | solution.py:877
  268.1 29.0 %collective-permute-start.26 = (bf16[1,512,384]{2,1,0:T(8,128)(2,1)S(1)}, bf16[1,512,384]{2,1,0:T(8,128)(2,1)S(1)}, u32[]{:S(2)}, u32[]{:S(2)}) collective-permute-start(bf16[1,512,384]{2,1,0:T(8,128)(2,1)S(1)} %shard_map.216), channel_id=1, source_target_pairs={{0,2},{1,3},{2,0},{3,1},{4,6},{5,7},{6,4},{7,5},{8,10},{9,11},{10,... | collective-permute-start | bytes 1179656 | tf_op jit(solution)/shard_map/ppermute | solution.py:877
  268.2 41.7 %collective-permute-start.14 = (bf16[1,256,384]{2,1,0:T(8,128)(2,1)S(1)}, bf16[1,256,384]{2,1,0:T(8,128)(2,1)S(1)}, u32[]{:S(2)}, u32[]{:S(2)}) collective-permute-start(bf16[1,256,384]{2,1,0:T(8,128)(2,1)S(1)} %shard_map.211), channel_id=1, source_target_pairs={{0,2},{1,3},{2,0},{3,1},{4,6},{5,7},{6,4},{7,5},{8,10},{9,11},{10,... | collective-permute-start | bytes 589832 | tf_op jit(solution)/shard_map/ppermute | solution.py:877
  278.1 36.7 %collective-permute-start.37 = (bf16[192,256]{1,0:T(8,128)(2,1)}, bf16[192,256]{1,0:T(8,128)(2,1)S(1)}, u32[]{:S(2)}, u32[]{:S(2)}) collective-permute-start(bf16[192,256]{1,0:T(8,128)(2,1)} %get-tuple-element.116), channel_id=1, source_target_pairs={{0,1},{1,0},{2,3},{3,2},{4,5},{5,4},{6,7},{7,6},{8,9},{9,8},{10,11... | collective-permute-start | bytes 294920 | tf_op jit(solution)/shard_map/ppermute | solution.py:835
  295.6 19.2 %collective-permute-start.38 = (bf16[192,256]{1,0:T(8,128)(2,1)}, bf16[192,256]{1,0:T(8,128)(2,1)S(1)}, u32[]{:S(2)}, u32[]{:S(2)}) collective-permute-start(bf16[192,256]{1,0:T(8,128)(2,1)} %get-tuple-element.116), channel_id=1, source_target_pairs={{0,2},{1,3},{2,0},{3,1},{4,6},{5,7},{6,4},{7,5},{8,10},{9,11},{10,... | collective-permute-start | bytes 294920 | tf_op jit(solution)/shard_map/ppermute | solution.py:835
  297.1 17.8 %collective-permute-start.39 = (bf16[192,256]{1,0:T(8,128)(2,1)}, bf16[192,256]{1,0:T(8,128)(2,1)S(1)}, u32[]{:S(2)}, u32[]{:S(2)}) collective-permute-start(bf16[192,256]{1,0:T(8,128)(2,1)} %get-tuple-element.116), channel_id=1, source_target_pairs={{0,3},{1,2},{2,1},{3,0},{4,7},{5,6},{6,5},{7,4},{8,11},{9,10},{10,... | collective-permute-start | bytes 294920 | tf_op jit(solution)/shard_map/ppermute | solution.py:835
  (67 other events, 1007.2 us)
